TPU v7x, 32 devices: a whole 2x2x4 slice. The times are simulated.
32 devices in a mesh: vir: 8 (over z, y), fit: 4 (over x, core).
Axes of the slice: x: 2, y: 2, z: 4, core: 2. Of those that a mesh axis runs over, the one named last changes fastest.
Arguments:
- fitted: bfloat16 [2, 2400, 24, 7168], P(None, 'vir', None, 'fit'), may hold values from -0.0234375 to 0.0234375
- vcouple: bfloat16 [2, 2400, 2400], P(None, 'fit'), may hold values from -0.125 to 0.125
- actfock: float32 [2, 24, 24], replicated, may hold values from -1.25 to 1.25
- eps_vir: float32 [2400], P('vir'), may hold values from 0.5 to 4
- eps_act: float32 [24], replicated, may hold values from -0.5 to 0.5
- pair_energy: float32 [64], replicated, may hold values from -3 to -2
- source: float32 [2, 2400, 1536], P(None, 'vir'), may hold values from -6 to 6
Outputs:
- amplitude: float32 [2, 2400, 1536], P(None, 'vir')
All inputs are finite; a program needn't handle non-finite values.
Results may differ from a plain program's by a relative error of at most 0.0026.
Values may be sent and summed in bfloat16 or wider, within the bound.
A program may use at most 256 MiB of HBM per device.

v0:
```python
import jax
import jax.numpy as jnp
from jax import lax
from jax.experimental import pallas as pl
from jax.experimental.pallas import tpu as pltpu
from jax.sharding import PartitionSpec as P

PASSES = 3
CHUNKS = 3
SLOTS = 3
BF16 = jnp.bfloat16
F32 = jnp.float32
MESH = pl.DeviceIdType.MESH

def contract_first(left, right):
    return lax.dot_general(
        left, right, (((0,), (0,)), ((), ())), preferred_element_type=jnp.float32
    )


def plain_product(left, right):
    return jnp.dot(left, right, preferred_element_type=jnp.float32)


def active_coupling(values, actfock, active, pairs):
    highest = lax.Precision.HIGHEST
    local_vir = values.shape[1]
    grid = values.reshape(2, local_vir, active, pairs)
    act_real = jnp.einsum("aup,ut->atp", grid[0], actfock[0], precision=highest) - jnp.einsum(
        "aup,ut->atp", grid[1], actfock[1], precision=highest
    )
    act_imag = jnp.einsum("aup,ut->atp", grid[0], actfock[1], precision=highest) + jnp.einsum(
        "aup,ut->atp", grid[1], actfock[0], precision=highest
    )
    return jnp.stack([act_real, act_imag]).reshape(2, local_vir, actfock.shape[2] * pairs)


def plain_device(fitted, vcouple, actfock, eps_vir, eps_act, pair_energy, source):
    local_vir = fitted.shape[1]
    active = fitted.shape[2]
    local_fit = fitted.shape[3]
    pairs = pair_energy.shape[0]
    block_rows = vcouple.shape[1]
    width = local_vir * active
    fit_index = lax.axis_index("fit")
    denominator = (
        eps_vir[:, None, None] + eps_act[None, :, None] - pair_energy[None, None, :]
    ).reshape(local_vir, active * pairs)
    amplitude = source / denominator[None]
    fit_real = fitted[0].reshape(width, local_fit)
    fit_imag = fitted[1].reshape(width, local_fit)
    for pass_index in range(PASSES):
        rounded = amplitude.astype(jnp.bfloat16)
        flat_both = jnp.concatenate(
            [rounded[0].reshape(width, pairs), rounded[1].reshape(width, pairs)], axis=1
        )
        real_side = contract_first(fit_real, flat_both)
        imag_side = contract_first(fit_imag, flat_both)
        over_real = real_side[:, :pairs] + imag_side[:, pairs:]
        over_imag = real_side[:, pairs:] - imag_side[:, :pairs]
        intersection = lax.psum(jnp.concatenate([over_real, over_imag], axis=1), "vir").astype(
            jnp.bfloat16
        )
        real_out = plain_product(fit_real, intersection)
        imag_out = plain_product(fit_imag, intersection)
        sum_real = real_out[:, :pairs] - imag_out[:, pairs:]
        sum_imag = real_out[:, pairs:] + imag_out[:, :pairs]
        fitted_part = jnp.stack([sum_real, sum_imag]).reshape(2, local_vir, active * pairs)
        regrouped = lax.all_to_all(rounded, "vir", split_axis=2, concat_axis=1, tiled=True)
        window = lax.dynamic_slice_in_dim(regrouped, fit_index * block_rows, block_rows, 1)
        couple_real = contract_first(vcouple[0], window[0]) - contract_first(vcouple[1], window[1])
        couple_imag = contract_first(vcouple[1], window[0]) + contract_first(vcouple[0], window[1])
        coupled = jnp.stack([couple_real, couple_imag])
        returned = lax.all_to_all(coupled, "vir", split_axis=1, concat_axis=2, tiled=True)
        fitted_part = fitted_part + returned
        total = lax.psum(fitted_part, "fit")
        part_amplitude = amplitude
        active_term = active_coupling(amplitude, actfock, active, pairs)
        residual = source - denominator[None] * part_amplitude - active_term - total
        updated = part_amplitude + residual / denominator[None]
        amplitude = updated
    return amplitude


def turn(values, pairs):
    return jnp.concatenate([-values[..., pairs:], values[..., :pairs]], axis=-1)


def whole_vmem(count):
    return [pl.BlockSpec(memory_space=pltpu.VMEM)] * count


def prologue_kernel(n_fit, eps_ref, row_ref, source_ref, x_ref, src_ref, den_ref, joined, start):
    fit = lax.axis_index("fit")
    local_vir, active, lanes = joined.shape
    pairs = lanes // 2
    for t in range(active):
        cols = slice(t * pairs, (t + 1) * pairs)
        both = jnp.concatenate([source_ref[0, :, cols], source_ref[1, :, cols]], axis=1)
        joined[:, t, :] = both
        start[:, t, :] = both / (eps_ref[...] + row_ref[t : t + 1, :])
    pieces = x_ref.shape[0] * n_fit
    own = local_vir // pieces
    for c in range(x_ref.shape[0]):
        for j in range(n_fit):
            first = (c * n_fit + j) * own
            block = start[first : first + own]
            x_ref[c, j] = block.reshape(own * active, lanes).astype(BF16)
        first = (c * n_fit + fit) * own
        src_ref[c] = joined[pl.ds(first, own)].reshape(own * active, lanes)
        for i in range(own):
            den_ref[c, i * active : (i + 1) * active, :] = eps_ref[first + i] + row_ref[...]


def prologue(eps_vir, row, source, n_fit):
    local_vir = eps_vir.shape[0]
    active, lanes = row.shape
    piece = local_vir // (CHUNKS * n_fit) * active
    own = jax.ShapeDtypeStruct((CHUNKS, piece, lanes), F32)
    return pl.pallas_call(
        lambda *refs: prologue_kernel(n_fit, *refs),
        in_specs=whole_vmem(3),
        out_specs=whole_vmem(3),
        out_shape=[jax.ShapeDtypeStruct((CHUNKS, n_fit, piece, lanes), BF16), own, own],
        scratch_shapes=[pltpu.VMEM((local_vir, active, lanes), F32)] * 2,
        compiler_params=pltpu.CompilerParams(vmem_limit_bytes=40 * 2**20),
        name="prologue",
    )(eps_vir[:, None] * jnp.ones((1, lanes), F32), row, source)


def epilogue_kernel(eps_ref, row_ref, source_ref, change_ref, out_ref, wide):
    local_vir, active, lanes = wide.shape
    pairs = lanes // 2
    own = change_ref.shape[1] // active
    for k in range(change_ref.shape[0]):
        wide[k * own : (k + 1) * own] = change_ref[k].astype(F32).reshape(own, active, lanes)
    for t in range(0, active, 2):
        cols = slice(t * pairs, (t + 2) * pairs)
        den = eps_ref[...] + row_ref[:, cols]
        left = wide[:, t, :]
        right = wide[:, t + 1, :]
        real = jnp.concatenate([left[:, :pairs], right[:, :pairs]], axis=1)
        imag = jnp.concatenate([left[:, pairs:], right[:, pairs:]], axis=1)
        out_ref[0, :, cols] = source_ref[0, :, cols] / den + real
        out_ref[1, :, cols] = source_ref[1, :, cols] / den + imag


def epilogue(eps_vir, flat_row, source, change, active, lanes):
    local_vir = eps_vir.shape[0]
    return pl.pallas_call(
        epilogue_kernel,
        in_specs=whole_vmem(4),
        out_specs=pl.BlockSpec(memory_space=pltpu.VMEM),
        out_shape=jax.ShapeDtypeStruct(source.shape, F32),
        scratch_shapes=[pltpu.VMEM((local_vir, active, lanes), F32)],
        compiler_params=pltpu.CompilerParams(vmem_limit_bytes=40 * 2**20),
        name="epilogue",
    )(eps_vir[:, None] * jnp.ones((1, lanes), F32), flat_row, source, change)


def ring_of(vir, n):
    odd = vir % 2
    return (1 - odd) * (vir // 2) + odd * (n - 1 - vir // 2)


def vir_of(pos, n):
    pos = (pos + n) % n
    high = pos // (n // 2)
    return (1 - high) * (2 * pos) + high * (2 * (n - 1 - pos) + 1)


def choose_int(index, table):
    value = 0
    for key, entry in table.items():
        value = value + jnp.where(index == key, entry, 0)
    return value


def passes_kernel(
    n, f_ref, start_ref, couple_ref, src_ref, den_ref, act_ref, x_ref,
    buf, buf_sem, acc, part, parts, whole, inter, turned, ring, spread, rows, virtual,
    near, near_in, far, far_in, kept, amp,
    ring_send, ring_recv, part_send, part_recv, whole_send, whole_recv, init_sem,
    near_send, near_recv, far_send, far_recv, gx_send, gx_recv, gc_send, gc_recv, gr_send, gr_recv,
):
    vir, fit = lax.axis_index("vir"), lax.axis_index("fit")
    chunks, n_fit, tile, lanes = x_ref.shape
    pairs = lanes // 2
    tiles = chunks * n_fit
    band = lanes // n
    depth = acc.shape[1]
    active = virtual.shape[1]
    span = spread.shape[0] // active
    half = n // 2
    pos = ring_of(vir, n)
    sides = ((vir_of(pos + 1, n), 1), (vir_of(pos - 1, n), -1))
    x, core = fit // 2, fit % 2
    beside = x * 2 + (1 - core)
    across = (1 - x) * 2 + core
    order = ((1 - x) * 2 + (1 - core), beside, across, fit)
    split = (chunks + 1) // 2
    group = act_ref.shape[1]

    def fetch(row_tile, slot):
        row = pl.multiple_of(row_tile * tile, 8)
        return pltpu.make_async_copy(
            f_ref.at[:, pl.ds(row, tile), :], buf.at[slot], buf_sem.at[slot]
        )

    def remote(src, dst, send, recv, axis, peer):
        return pltpu.make_async_remote_copy(
            src_ref=src, dst_ref=dst, send_sem=send, recv_sem=recv,
            device_id={axis: peer}, device_id_type=MESH,
        )

    def back_tile(k):
        value = 0
        for j in range(n_fit):
            value = value + jnp.where(k == j, order[j], 0)
        return value

    for i in range(SLOTS - 1):
        fetch(i, i).start()
    inits = [
        pltpu.make_async_copy(start_ref.at[c], x_ref.at[c], init_sem.at[0, c]) for c in range(chunks)
    ] + [
        pltpu.make_async_copy(start_ref.at[c, fit], ring.at[0, vir, c], init_sem.at[1, c])
        for c in range(chunks)
    ]
    for init in inits:
        init.start()

    barrier = pltpu.get_barrier_semaphore()
    for k in range(1, n):
        pl.semaphore_signal(barrier, inc=1, device_id={"vir": (vir + k) % n}, device_id_type=MESH)
    for peer in (beside, across):
        pl.semaphore_signal(barrier, inc=1, device_id={"fit": peer}, device_id_type=MESH)

    for c in range(chunks):
        amp[c] = src_ref[c] / den_ref[c]
    spread[...] = jnp.zeros_like(spread)
    for init in inits:
        init.wait()
    pl.semaphore_wait(barrier, n + 1)

    def sent_last(side, c):
        return (c < split) if side == 0 else (c >= split)

    def hop(parity, side, stage, c):
        to, sign = sides[side]
        owner = vir_of(pos - sign * (stage - 1), n)
        slot = ring.at[parity, owner, c]
        return remote(
            slot, slot, ring_send.at[side, stage - 1, c], ring_recv.at[side, stage - 1, c], "vir", to
        )

    def lay(parity, owner, c):
        spread[0:tile, :] = ring[parity, owner, c].astype(F32)
        top = pl.multiple_of((c * n + owner) * span, span)
        for t in range(active):
            rows[pl.ds(top, span), t * lanes : (t + 1) * lanes] = spread[
                pl.ds(t, span, stride=active), :
            ].astype(BF16)

    def landed(parity, side, stage, c):
        to, sign = sides[side]
        owner = vir_of(pos - sign * stage, n)
        slot = ring.at[parity, owner, c]
        remote(
            slot, slot, ring_send.at[side, stage - 1, c], ring_recv.at[side, stage - 1, c], "vir", to
        ).wait_recv()
        return owner

    def open_ring(parity, c):
        for side in range(2):
            hop(parity, side, 1, c).start()

    def relay(parity, stage, c):
        owners = []
        for side in range(2):
            owners.append(landed(parity, side, stage, c))

            @pl.when((stage < half - 1) | sent_last(side, c))
            def _():
                hop(parity, side, stage + 1, c).start()

        for owner in owners:
            lay(parity, owner, c)

    def part_copy(k):
        peer = (vir + k) % n
        return remote(
            part.at[peer], parts.at[vir], part_send.at[k - 1], part_recv.at[k - 1], "vir", peer
        )

    def part_landed(k):
        peer = (vir + n - k) % n
        remote(
            part.at[peer], parts.at[peer], part_send.at[k - 1], part_recv.at[k - 1], "vir", peer
        ).wait_recv()
        return peer

    def whole_copy(k):
        peer = (vir + k) % n
        return remote(
            whole.at[vir], whole.at[vir], whole_send.at[k - 1], whole_recv.at[k - 1], "vir", peer
        )

    def whole_landed(k):
        peer = (vir + n - k) % n
        remote(
            whole.at[peer], whole.at[peer], whole_send.at[k - 1], whole_recv.at[k - 1], "vir", peer
        ).wait_recv()

    def near_copy(c, k):
        return remote(
            near.at[c, k], near_in.at[c, k], near_send.at[c, k], near_recv.at[c, k], "fit", beside
        )

    def far_copy(c):
        return remote(far.at[c], far_in.at[c], far_send.at[c], far_recv.at[c], "fit", across)

    def gather_across(c, owner):
        slot = x_ref.at[c, owner]
        return remote(slot, slot, gx_send.at[c], gx_recv.at[c], "fit", across)

    def gather_beside(c, owner):
        slot = x_ref.at[c, owner]
        return remote(slot, slot, gc_send.at[c], gc_recv.at[c], "fit", beside)

    def gather_relay(c, owner):
        slot = x_ref.at[c, owner]
        return remote(slot, slot, gr_send.at[c], gr_recv.at[c], "fit", beside)

    def update(c, parity, final):
        far_copy(c).wait_recv()

        def some(g, carry):
            cut = pl.ds(pl.multiple_of(g * group, 8), group)
            value = amp[c, cut, :]
            act = jnp.dot(
                act_ref[0], value, precision=lax.Precision.HIGHEST, preferred_element_type=F32
            ) + jnp.dot(
                act_ref[1], turn(value, pairs), precision=lax.Precision.HIGHEST,
                preferred_element_type=F32,
            )
            total = kept[c, cut, :] + far_in[c, cut, :].astype(F32)
            den = den_ref[c, cut, :]
            source = src_ref[c, cut, :]
            fresh = (source - act - total) / den
            amp[c, cut, :] = fresh
            kept[c, cut, :] = fresh - jnp.where(final, source / den, 0.0)
            return carry

        lax.fori_loop(0, tile // group, some, 0)
        out = kept[c].astype(BF16)
        x_ref[c, fit] = out
        gather_across(c, fit).start()
        gather_beside(c, fit).start()

        @pl.when(jnp.logical_not(final))
        def _():
            ring[parity, vir, c] = out
            open_ring(parity, c)

    def pass_on(c):
        gather_across(c, across).wait_recv()
        gather_relay(c, across).start()

    def gathered(c):
        gather_beside(c, beside).wait_recv()
        gather_relay(c, order[0]).wait_recv()

    def back_sends(c):
        for k in range(2):
            near_copy(c, k).wait_send()
        far_copy(c).wait_send()
        gather_across(c, fit).wait_send()
        gather_beside(c, fit).wait_send()
        gather_relay(c, across).wait_send()

    for c in range(chunks):
        open_ring(0, c)

    contract = (((0,), (0,)), ((), ()))
    last_chunk = chunks - 1

    def one_pass(p, carry):
        parity = lax.rem(p, 2)
        later = p > 0
        acc[...] = jnp.zeros_like(acc)

        def contract_step(i, carry):
            ahead = i + SLOTS - 1
            inside = ahead < tiles
            target = jnp.where(inside, ahead, back_tile(ahead - tiles))
            fetch(target, lax.rem(ahead, SLOTS)).start()
            c = i // n_fit
            j = lax.rem(i, n_fit)

            @pl.when(later & (j == 0))
            def _():
                gathered(c)

            slot = lax.rem(i, SLOTS)
            fetch(i, slot).wait()
            values = x_ref[c, j]
            acc[...] += lax.dot_general(
                values, buf[slot, 0], contract, preferred_element_type=F32
            ) + lax.dot_general(
                -turn(values, pairs), buf[slot, 1], contract, preferred_element_type=F32
            )

            @pl.when(later & (i == 2))
            def _():
                update(last_chunk, parity, False)

            @pl.when(later & ((i == 1) | (i == 5)))
            def _():
                pass_on(jnp.where(i == 1, last_chunk - 1, last_chunk))

            code = jnp.where(later, choose_int(i, LATER_RELAYS), choose_int(i, FIRST_RELAYS))

            @pl.when(code > 0)
            def _():
                relay(parity, code // 8, lax.rem(code, 8))

            return carry

        lax.fori_loop(0, tiles, contract_step, 0)

        for k in range(n):
            part[k] = acc[k * band : (k + 1) * band, :].astype(BF16)
        for k in range(1, n):
            part_copy(k).start()

        @pl.when(later)
        def _():
            for c in range(chunks):
                back_sends(c)

        for c in range(chunks):
            lay(parity, vir, c)
        for c in range(chunks):
            lay(parity, landed(parity, 0 if c < split else 1, half, c), c)
        total = acc[pl.ds(pl.multiple_of(vir * band, band), band), :]
        for k in range(1, n):
            total = total + parts[part_landed(k)].astype(F32)
        whole[vir] = total.astype(BF16)
        for k in range(1, n):
            whole_copy(k).start()

        for t in range(0, active, 2):
            left = rows[:, t * lanes : (t + 1) * lanes]
            right = rows[:, (t + 1) * lanes : (t + 2) * lanes]
            plain = jnp.concatenate([left, right], axis=1)
            other = jnp.concatenate([turn(left, pairs), turn(right, pairs)], axis=1)
            value = plain_product(couple_ref[0], plain) + plain_product(couple_ref[1], other)
            virtual[:, t, :] = value[:, :lanes]
            virtual[:, t + 1, :] = value[:, lanes:]

        for c in range(chunks):
            for side in range(2):
                for stage in range(1, half + 1):
                    if stage < half or sent_last(side, c):
                        hop(parity, side, stage, c).wait_send()
        for k in range(1, n):
            whole_landed(k)
        block = depth
        for width in (512, 384, 256, 128):
            if depth % width == 0:
                block = width
                break
        for q in range(0, depth, block):
            cols = whole[:, :, q : q + block].reshape(lanes, block).astype(F32).T
            inter[q : q + block, :] = cols.astype(BF16)
            turned[q : q + block, :] = turn(cols, pairs).astype(BF16)
        for k in range(1, n):
            part_copy(k).wait_send()
            whole_copy(k).wait_send()

        final = p == PASSES - 1
        own = tile // active

        def back_chunk(c, carry):
            for k in range(n_fit):
                i = c * n_fit + k
                ahead = i + SLOTS - 1
                inside = ahead < tiles
                after = ahead - tiles
                target = jnp.where(
                    inside, (ahead // n_fit) * n_fit + order[(k + SLOTS - 1) % n_fit], after
                )

                @pl.when(inside | jnp.logical_not(final))
                def _():
                    fetch(target, lax.rem(ahead, SLOTS)).start()

                slot = lax.rem(i, SLOTS)
                where = c * n_fit + order[k]
                fetch(where, slot).wait()
                value = (
                    plain_product(buf[slot, 0], inter[...])
                    + plain_product(buf[slot, 1], turned[...])
                    + virtual[pl.ds(where * own, own)].reshape(tile, lanes)
                )
                if k < 2:
                    near[c, k] = value.astype(BF16)
                    near_copy(c, k).start()
                elif k == 2:
                    near_copy(c, 0).wait_recv()
                    far[c] = (value + near_in[c, 0].astype(F32)).astype(BF16)
                    far_copy(c).start()
                else:
                    near_copy(c, 1).wait_recv()
                    kept[c] = value + near_in[c, 1].astype(F32)
                if k == 0:

                    @pl.when(c >= 2)
                    def _():
                        pass_on(c - 2)

                    @pl.when((c >= 2) & jnp.logical_not(final))
                    def _():
                        relay(1 - parity, 1, c - 2)

                if k == 1:

                    @pl.when(c >= 1)
                    def _():
                        update(c - 1, 1 - parity, final)

                if k == 3:

                    @pl.when((c >= 2) & jnp.logical_not(final))
                    def _():
                        relay(1 - parity, 2, c - 2)

            return carry

        lax.fori_loop(0, chunks, back_chunk, 0)
        return carry

    lax.fori_loop(0, PASSES, one_pass, 0)
    pass_on(last_chunk - 1)
    update(last_chunk, 0, True)
    pass_on(last_chunk)
    for c in range(chunks):
        gathered(c)
        back_sends(c)


FIRST_RELAYS = {1: 8, 2: 9, 3: 10, 5: 16, 6: 17, 7: 18, 9: 24, 10: 25, 11: 26}
LATER_RELAYS = {0: 9, 3: 24, 4: 17, 6: 10, 7: 25, 8: 18, 10: 26}


def all_passes(fit_rows, values, couple, src, den, act, active, n):
    depth = fit_rows.shape[2]
    chunks, n_fit, tile, lanes = values.shape
    local_vir, wide = couple.shape[1:]
    span = wide // (chunks * n)
    half = n // 2
    dma = pltpu.SemaphoreType.DMA
    band = pltpu.VMEM((n, lanes // n, depth), BF16)
    each = pltpu.VMEM((chunks, tile, lanes), BF16)
    twice = pltpu.VMEM((chunks, 2, tile, lanes), BF16)
    state = pltpu.VMEM((chunks, tile, lanes), F32)
    return pl.pallas_call(
        lambda *refs: passes_kernel(n, *refs),
        in_specs=[pl.BlockSpec(memory_space=pl.ANY)] + whole_vmem(5),
        out_specs=pl.BlockSpec(memory_space=pltpu.VMEM),
        out_shape=jax.ShapeDtypeStruct((chunks, n_fit, tile, lanes), BF16),
        scratch_shapes=[
            pltpu.VMEM((SLOTS, 2, tile, depth), BF16),
            dma((SLOTS,)),
            pltpu.VMEM((lanes, depth), F32),
            band,
            band,
            band,
            pltpu.VMEM((depth, lanes), BF16),
            pltpu.VMEM((depth, lanes), BF16),
            pltpu.VMEM((2, n, chunks, tile, lanes), BF16),
            pltpu.VMEM((span * active, lanes), F32),
            pltpu.VMEM((wide, active * lanes), BF16),
            pltpu.VMEM((local_vir, active, lanes), F32),
            twice,
            twice,
            each,
            each,
            state,
            state,
            dma((2, half, chunks)),
            dma((2, half, chunks)),
        ]
        + [dma((n - 1,))] * 4
        + [dma((2, chunks))]
        + [dma((chunks, 2))] * 2
        + [dma((chunks,))] * 8,
        compiler_params=pltpu.CompilerParams(
            collective_id=0, has_side_effects=True, vmem_limit_bytes=60 * 2**20
        ),
        name="passes",
    )(fit_rows, values, couple, src, den, act)


def per_device(fitted, vcouple, actfock, eps_vir, eps_act, pair_energy, source):
    n_fit, n_vir = lax.axis_size("fit"), lax.axis_size("vir")
    vir_index = lax.axis_index("vir")
    local_vir, active, local_fit = fitted.shape[1:]
    block_rows = vcouple.shape[1]
    pairs = pair_energy.shape[0]
    lanes = 2 * pairs
    own = local_vir // (CHUNKS * n_fit)
    span = -(-own // 16) * 16
    held = block_rows // local_vir

    row = eps_act[:, None] - pair_energy[None, :]
    wide_row = jnp.concatenate([row, row], axis=1)
    values, src, den = prologue(eps_vir, wide_row, source, n_fit)

    couple = lax.dynamic_slice_in_dim(vcouple, vir_index * local_vir, local_vir, 2)
    couple = couple.reshape(2, held, CHUNKS, n_fit, own, local_vir).transpose(3, 0, 1, 2, 4, 5)
    couple = couple.reshape(n_fit, 2 * held * CHUNKS * own, local_vir)
    couple = lax.all_to_all(couple, "fit", 0, 0)
    couple = couple.reshape(n_fit, 2, held, CHUNKS, own, local_vir).transpose(1, 5, 3, 0, 2, 4)
    couple = jnp.pad(couple, ((0, 0),) * 5 + ((0, span - own),))
    couple = couple.reshape(2, local_vir, CHUNKS * n_vir * span)

    group = 5
    eye = jnp.eye(group, dtype=F32)
    act = jnp.einsum("gh,cut->cgthu", eye, actfock).reshape(2, group * active, group * active)
    fit_rows = fitted.reshape(2, local_vir * active, local_fit)
    values = all_passes(fit_rows, values, couple, src, den, act, active, n_vir)
    change = values.reshape(CHUNKS * n_fit, own * active, lanes)
    return epilogue(eps_vir, row.reshape(1, active * pairs), source, change, active, lanes)


def choose(mesh):
    def body(*args):
        n_fit, n_vir = mesh.shape["fit"], mesh.shape["vir"]
        fitted, vcouple, actfock, eps_vir, eps_act, pair_energy, source = args
        local_vir, active, local_fit = fitted.shape[1:]
        fits = (
            n_fit == 4
            and CHUNKS == 3
            and n_vir == 8
            and n_vir % 2 == 0
            and 2 * pair_energy.shape[0] == 128
            and n_vir * 16 == 128
            and local_vir % (CHUNKS * n_fit * 5) == 0
            and vcouple.shape[1] % local_vir == 0
            and active % 8 == 0
            and local_fit % 128 == 0
        )
        return per_device(*args) if fits else plain_device(*args)

    return body


def solution(mesh):
    return jax.shard_map(
        choose(mesh),
        mesh=mesh,
        in_specs=(
            P(None, "vir", None, "fit"),
            P(None, "fit", None),
            P(),
            P("vir"),
            P(),
            P(),
            P(None, "vir", None),
        ),
        out_specs=P(None, "vir", None),
        check_vma=False,
    )
```

profile of v0, /device:TPU:0, one launch (start us, length us, event | category | flops | bytes accessed | tf_op | source)
XLA Modules:
  0.0 285.7 jit_solution(6299188150890205364)
XLA Ops:
  0.0 1.7 constant_dynamic-slice_fusion
  1.7 0.7 copy.21
  2.4 0.4 copy.22
  2.8 1.1 copy.23
  3.9 4.2 %all-to-all-start = ((bf16[4,300,300]{2,1,0:T(8,128)(2,1)}), bf16[4,300,300]{2,1,0:T(8,128)(2,1)S(1)}, u32[]{:S(2)}, u32[]{:S(2)}) async-start(bf16[4,300,300]{2,1,0:T(8,128)(2,1)} %copy.23), calls=%async_computation | async-start | bytes 1867776 | tf_op jit(solution)/shard_map/all_to_all | solution.py:624
  8.2 0.1 sub.26.row_ref
  8.3 0.1 multiply_bitcast_fusion
  8.5 0.8 reshape.52.refs_5_
  9.3 2.8 copy.28.refs_2_.source_ref
  12.1 0.1 pad_maximum_fusion.refs_1_
  12.2 0.1 mul.4.refs_0_.eps_ref
  12.3 5.0 %prologue.1 = (bf16[3,4,600,128]{3,2,1,0:T(8,128)(2,1)S(1)}, f32[3,600,128]{2,1,0:T(8,128)S(1)}, f32[3,600,128]{2,1,0:T(8,128)S(1)}) custom-call(f32[300,128]{1,0:T(8,128)S(1)} %mul.4.refs_0_.eps_ref, f32[24,128]{1,0:T(8,128)S(1)} %pad_maximum_fusion.refs_1_, f32[2,300,1536]{2,1,0:T(8,128)S(1)} %copy.28.refs_2_.source_ref), custom_call_target="tpu_custom_call" | custom-call | tf_op jit(solution)/shard_map/prologue/pallas_call | solution.py:120
  17.3 1.8 copy-done
  19.1 1.2 copy-done.3
  20.4 0.9 copy-done.4
  21.3 1.0 copy-done.5
  22.3 0.4 copy.24
  22.7 0.2 copy.30
  22.9 0.2 pad.4.clone
  23.1 1.4 copy.27.refs_2_
  24.4 252.3 %passes.1 = bf16[3,4,600,128]{3,2,1,0:T(8,128)(2,1)} custom-call(bf16[2,7200,1792]{2,1,0:T(8,128)(2,1)} %bitcast.13, bf16[3,4,600,128]{3,2,1,0:T(8,128)(2,1)} %copy-done.3, bf16[2,300,768]{2,1,0:T(8,128)(2,1)} %copy.27.refs_2_, f32[3,600,128]{2,1,0:T(8,128)} %copy-done.4, f32[3,600,128]{2,1,0:T(8,128)} %copy-done.5, f32[2,120,120]{2,1,0:T(8,128)} %reshape.52.refs_5_), custom_call_target="tpu_custom_call" | custom-call | tf_op jit(solution)/shard_map/passes/pallas_call | solution.py:568
  276.8 1.5 copy-done.2
  278.3 2.8 epilogue.1
  281.0 4.7 %copy.29 = f32[2,300,1536]{2,0,1:T(2,128)} copy(f32[2,300,1536]{2,1,0:T(8,128)S(1)} %epilogue.1) | data formatting | bytes 7372800 | tf_op jit(solution)/shard_map/epilogue/pallas_call | solution.py:150
  (19 shorter events, 0.2 us)
Async XLA Ops:
  1.7 6.4 %copy-start.8 = (f32[64]{0:T(128)S(1)}, f32[64]{0:T(128)}, u32[]{:S(2)}) copy-start(f32[64]{0:T(128)} %param.12) | copy-start | bytes 772
  1.7 6.4 %copy-start.9 = (f32[24]{0:T(128)S(1)}, f32[24]{0:T(128)}, u32[]{:S(2)}) copy-start(f32[24]{0:T(128)} %param.11) | copy-start | bytes 292
  1.7 6.6 %copy-start.6 = (f32[2,24,24]{2,1,0:T(8,128)S(1)}, f32[2,24,24]{2,1,0:T(8,128)}, u32[]{:S(2)}) copy-start(f32[2,24,24]{2,1,0:T(8,128)} %param.9) | copy-start | bytes 13828
  3.9 18.4 %all-to-all-start = ((bf16[4,300,300]{2,1,0:T(8,128)(2,1)}), bf16[4,300,300]{2,1,0:T(8,128)(2,1)S(1)}, u32[]{:S(2)}, u32[]{:S(2)}) async-start(bf16[4,300,300]{2,1,0:T(8,128)(2,1)} %copy.23), calls=%async_computation | async-start | bytes 1867776 | tf_op jit(solution)/shard_map/all_to_all | solution.py:624
  9.3 2.8 copy-start.7
  17.3 1.8 copy-start
  19.1 1.2 copy-start.3
  20.4 0.9 copy-start.4
  21.3 1.0 copy-start.5
  24.4 252.3 %copy-start.1 = (f32[2,300,1536]{2,1,0:T(8,128)S(1)}, f32[2,300,1536]{2,1,0:T(8,128)}, u32[]{:S(2)}) copy-start(f32[2,300,1536]{2,1,0:T(8,128)} %copy-done) | copy-start | bytes 11059204
  276.8 1.5 copy-start.2
where the time goes:
time: 287 us; the launch traced here: 286 us
  Pallas kernels  260 us (91%)
  local copies, waits for them, and re-layouts  21 us (7%)
  starting transfers between devices  4.24 us (1%)
    pallas_call x1, Pallas kernels, all_passes(): pl.pallas_call(lambda *refs: passes_kernel(n, *refs), in_specs=[pl.BlockS...  252 us
    unnamed x23, local copies, waits for them, and re-layouts  9.53 us
  transfers between devices with their start and end apart: 1, of which 0 were waited for; matrix products, arithmetic and copies ran while one was open for 1% of the time, Pallas kernels for 2%

commit v1 on v0

--- a/solution.py
+++ b/solution.py
@@ -90,72 +90,44 @@
     return [pl.BlockSpec(memory_space=pltpu.VMEM)] * count
 
 
-def prologue_kernel(n_fit, eps_ref, row_ref, source_ref, x_ref, src_ref, den_ref, joined, start):
-    fit = lax.axis_index("fit")
-    local_vir, active, lanes = joined.shape
-    pairs = lanes // 2
-    for t in range(active):
-        cols = slice(t * pairs, (t + 1) * pairs)
-        both = jnp.concatenate([source_ref[0, :, cols], source_ref[1, :, cols]], axis=1)
-        joined[:, t, :] = both
-        start[:, t, :] = both / (eps_ref[...] + row_ref[t : t + 1, :])
-    pieces = x_ref.shape[0] * n_fit
-    own = local_vir // pieces
-    for c in range(x_ref.shape[0]):
-        for j in range(n_fit):
-            first = (c * n_fit + j) * own
-            block = start[first : first + own]
-            x_ref[c, j] = block.reshape(own * active, lanes).astype(BF16)
-        first = (c * n_fit + fit) * own
-        src_ref[c] = joined[pl.ds(first, own)].reshape(own * active, lanes)
-        for i in range(own):
-            den_ref[c, i * active : (i + 1) * active, :] = eps_ref[first + i] + row_ref[...]
-
-
-def prologue(eps_vir, row, source, n_fit):
-    local_vir = eps_vir.shape[0]
-    active, lanes = row.shape
-    piece = local_vir // (CHUNKS * n_fit) * active
-    own = jax.ShapeDtypeStruct((CHUNKS, piece, lanes), F32)
-    return pl.pallas_call(
-        lambda *refs: prologue_kernel(n_fit, *refs),
-        in_specs=whole_vmem(3),
-        out_specs=whole_vmem(3),
-        out_shape=[jax.ShapeDtypeStruct((CHUNKS, n_fit, piece, lanes), BF16), own, own],
-        scratch_shapes=[pltpu.VMEM((local_vir, active, lanes), F32)] * 2,
-        compiler_params=pltpu.CompilerParams(vmem_limit_bytes=40 * 2**20),
-        name="prologue",
-    )(eps_vir[:, None] * jnp.ones((1, lanes), F32), row, source)
-
-
-def epilogue_kernel(eps_ref, row_ref, source_ref, change_ref, out_ref, wide):
-    local_vir, active, lanes = wide.shape
-    pairs = lanes // 2
-    own = change_ref.shape[1] // active
-    for k in range(change_ref.shape[0]):
-        wide[k * own : (k + 1) * own] = change_ref[k].astype(F32).reshape(own, active, lanes)
-    for t in range(0, active, 2):
-        cols = slice(t * pairs, (t + 2) * pairs)
-        den = eps_ref[...] + row_ref[:, cols]
-        left = wide[:, t, :]
-        right = wide[:, t + 1, :]
-        real = jnp.concatenate([left[:, :pairs], right[:, :pairs]], axis=1)
-        imag = jnp.concatenate([left[:, pairs:], right[:, pairs:]], axis=1)
-        out_ref[0, :, cols] = source_ref[0, :, cols] / den + real
-        out_ref[1, :, cols] = source_ref[1, :, cols] / den + imag
-
-
-def epilogue(eps_vir, flat_row, source, change, active, lanes):
-    local_vir = eps_vir.shape[0]
+def mix(values, pairs):
+    rows, lanes = values.shape
+    even = lax.broadcasted_iota(jnp.int32, (rows, lanes), 0) % 2 == 0
+    low = lax.broadcasted_iota(jnp.int32, (rows, lanes), 1) < pairs
+    other = pltpu.roll(values, pairs, 1)
+    up = pltpu.roll(other, rows - 1, 0)
+    down = pltpu.roll(other, 1, 0)
+    return jnp.where(even == low, values, jnp.where(even, up, down))
+
+
+def epilogue_kernel(eps_ref, row_ref, source_ref, change_ref, out_ref, den):
+    tile, lanes = source_ref.shape
+    active = row_ref.shape[0]
+    own = tile // active
+    first = pl.program_id(0) * own
+    for i in range(own):
+        den[i * active : (i + 1) * active, :] = eps_ref[pl.ds(first + i, 1), :] + row_ref[...]
+    start = mix(source_ref[...], lanes // 2) / den[...]
+    out_ref[...] = mix(start + change_ref[0].astype(F32), lanes // 2)
+
+
+def epilogue(eps, row, source, change):
+    pieces, tile, lanes = change.shape
     return pl.pallas_call(
         epilogue_kernel,
-        in_specs=whole_vmem(4),
-        out_specs=pl.BlockSpec(memory_space=pltpu.VMEM),
+        grid=(pieces,),
+        in_specs=[
+            pl.BlockSpec(eps.shape, lambda i: (0, 0)),
+            pl.BlockSpec(row.shape, lambda i: (0, 0)),
+            pl.BlockSpec((tile, lanes), lambda i: (i, 0)),
+            pl.BlockSpec((1, tile, lanes), lambda i: (i, 0, 0)),
+        ],
+        out_specs=pl.BlockSpec((tile, lanes), lambda i: (i, 0)),
         out_shape=jax.ShapeDtypeStruct(source.shape, F32),
-        scratch_shapes=[pltpu.VMEM((local_vir, active, lanes), F32)],
-        compiler_params=pltpu.CompilerParams(vmem_limit_bytes=40 * 2**20),
+        scratch_shapes=[pltpu.VMEM((tile, lanes), F32)],
+        compiler_params=pltpu.CompilerParams(vmem_limit_bytes=16 * 2**20),
         name="epilogue",
-    )(eps_vir[:, None] * jnp.ones((1, lanes), F32), flat_row, source, change)
+    )(eps, row, source, change)
 
 
 def ring_of(vir, n):
@@ -177,10 +149,11 @@
 
 
 def passes_kernel(
-    n, f_ref, start_ref, couple_ref, src_ref, den_ref, act_ref, x_ref,
+    n, f_ref, source_ref, give_ref, eps_ref, row_ref, act_ref, x_ref,
     buf, buf_sem, acc, part, parts, whole, inter, turned, ring, spread, rows, virtual,
-    near, near_in, far, far_in, kept, amp,
+    near, near_in, far, far_in, kept, amp, src, inverse, base, raw, den, couple,
     ring_send, ring_recv, part_send, part_recv, whole_send, whole_recv, init_sem,
+    couple_send, couple_recv,
     near_send, near_recv, far_send, far_recv, gx_send, gx_recv, gc_send, gc_recv, gr_send, gr_recv,
 ):
     vir, fit = lax.axis_index("vir"), lax.axis_index("fit")
@@ -221,27 +194,48 @@
 
     for i in range(SLOTS - 1):
         fetch(i, i).start()
-    inits = [
-        pltpu.make_async_copy(start_ref.at[c], x_ref.at[c], init_sem.at[0, c]) for c in range(chunks)
-    ] + [
-        pltpu.make_async_copy(start_ref.at[c, fit], ring.at[0, vir, c], init_sem.at[1, c])
+    own = tile // active
+    raw_copies = [
+        pltpu.make_async_copy(
+            source_ref.at[pl.ds(pl.multiple_of((c * n_fit + fit) * tile, 8), tile), :],
+            src.at[c], init_sem.at[0, c],
+        )
         for c in range(chunks)
     ]
-    for init in inits:
-        init.start()
+    for copy in raw_copies:
+        copy.start()
+    bulk = pltpu.make_async_copy(source_ref, raw, init_sem.at[1, 0])
+    bulk.start()
+    own_couple = pltpu.make_async_copy(give_ref.at[fit], couple.at[fit], init_sem.at[1, 1])
+    own_couple.start()
 
     barrier = pltpu.get_barrier_semaphore()
     for k in range(1, n):
         pl.semaphore_signal(barrier, inc=1, device_id={"vir": (vir + k) % n}, device_id_type=MESH)
-    for peer in (beside, across):
-        pl.semaphore_signal(barrier, inc=1, device_id={"fit": peer}, device_id_type=MESH)
-
-    for c in range(chunks):
-        amp[c] = src_ref[c] / den_ref[c]
+    for k in range(1, n_fit):
+        pl.semaphore_signal(
+            barrier, inc=1, device_id={"fit": (fit + k) % n_fit}, device_id_type=MESH
+        )
+
+    def fill(first):
+        for i in range(own):
+            den[i * active : (i + 1) * active, :] = eps_ref[pl.ds(first + i, 1), :] + row_ref[...]
+
+    def begin(c, carry):
+        fill((c * n_fit + fit) * own)
+        source = mix(src[c], pairs)
+        start = source / den[...]
+        src[c] = source
+        inverse[c] = 1.0 / den[...]
+        amp[c] = start
+        ring[0, vir, c] = start.astype(BF16)
+        return carry
+
+    for copy in raw_copies:
+        copy.wait()
+    lax.fori_loop(0, chunks, begin, 0)
     spread[...] = jnp.zeros_like(spread)
-    for init in inits:
-        init.wait()
-    pl.semaphore_wait(barrier, n + 1)
+    pl.semaphore_wait(barrier, n + n_fit - 2)
 
     def sent_last(side, c):
         return (c < split) if side == 0 else (c >= split)
@@ -256,7 +250,7 @@
 
     def lay(parity, owner, c):
         spread[0:tile, :] = ring[parity, owner, c].astype(F32)
-        top = pl.multiple_of((c * n + owner) * span, span)
+        top = pl.multiple_of((owner * chunks + c) * span, span)
         for t in range(active):
             rows[pl.ds(top, span), t * lanes : (t + 1) * lanes] = spread[
                 pl.ds(t, span, stride=active), :
@@ -335,25 +329,10 @@
     def update(c, parity, final):
         far_copy(c).wait_recv()
 
-        def some(g, carry):
-            cut = pl.ds(pl.multiple_of(g * group, 8), group)
-            value = amp[c, cut, :]
-            act = jnp.dot(
-                act_ref[0], value, precision=lax.Precision.HIGHEST, preferred_element_type=F32
-            ) + jnp.dot(
-                act_ref[1], turn(value, pairs), precision=lax.Precision.HIGHEST,
-                preferred_element_type=F32,
-            )
-            total = kept[c, cut, :] + far_in[c, cut, :].astype(F32)
-            den = den_ref[c, cut, :]
-            source = src_ref[c, cut, :]
-            fresh = (source - act - total) / den
-            amp[c, cut, :] = fresh
-            kept[c, cut, :] = fresh - jnp.where(final, source / den, 0.0)
-            return carry
-
-        lax.fori_loop(0, tile // group, some, 0)
-        out = kept[c].astype(BF16)
+        total = kept[c] + far_in[c].astype(F32)
+        fresh = (base[c] - total) * inverse[c]
+        amp[c] = fresh
+        out = (fresh - jnp.where(final, src[c] * inverse[c], 0.0)).astype(BF16)
         x_ref[c, fit] = out
         gather_across(c, fit).start()
         gather_beside(c, fit).start()
@@ -381,6 +360,52 @@
 
     for c in range(chunks):
         open_ring(0, c)
+
+    def couple_copy(k):
+        peer = (fit + k) % n_fit
+        return remote(
+            give_ref.at[peer], couple.at[fit], couple_send.at[k - 1], couple_recv.at[k - 1], "fit", peer
+        )
+
+    def couple_landed(k):
+        peer = (fit + n_fit - k) % n_fit
+        remote(
+            give_ref.at[peer], couple.at[peer], couple_send.at[k - 1], couple_recv.at[k - 1], "fit", peer
+        ).wait_recv()
+
+    for k in range(1, n_fit):
+        couple_copy(k).start()
+
+    def spread_start(i, carry):
+        fill(i * own)
+        source = raw[pl.ds(pl.multiple_of(i * tile, 8), tile), :]
+        x_ref[i // n_fit, lax.rem(i, n_fit)] = (mix(source, pairs) / den[...]).astype(BF16)
+        return carry
+
+    bulk.wait()
+    lax.fori_loop(0, tiles, spread_start, 0)
+
+    def active_base(c, carry):
+        value = amp[c]
+        cuts = [value[g : g + group] for g in range(0, tile, group)]
+        both = jnp.concatenate(
+            [
+                jnp.concatenate(cuts, axis=1),
+                jnp.concatenate([turn(cut, pairs) for cut in cuts], axis=1),
+            ],
+            axis=0,
+        )
+        high = both.astype(BF16)
+        low = (both - high.astype(F32)).astype(BF16)
+        act = (
+            plain_product(act_ref[0], high)
+            + plain_product(act_ref[0], low)
+            + plain_product(act_ref[1], high)
+        )
+        for g in range(tile // group):
+            cut = slice(g * group, (g + 1) * group)
+            base[c, cut, :] = src[c, cut, :] - act[:, g * lanes : (g + 1) * lanes]
+        return carry
 
     contract = (((0,), (0,)), ((), ()))
     last_chunk = chunks - 1
@@ -441,23 +466,36 @@
 
         for c in range(chunks):
             lay(parity, vir, c)
-        for c in range(chunks):
-            lay(parity, landed(parity, 0 if c < split else 1, half, c), c)
+        lax.fori_loop(0, chunks, active_base, 0)
+
+        @pl.when(jnp.logical_not(later))
+        def _():
+            own_couple.wait()
+            for k in range(1, n_fit):
+                couple_landed(k)
+
         total = acc[pl.ds(pl.multiple_of(vir * band, band), band), :]
         for k in range(1, n):
             total = total + parts[part_landed(k)].astype(F32)
         whole[vir] = total.astype(BF16)
         for k in range(1, n):
             whole_copy(k).start()
+        for c in range(chunks):
+            lay(parity, landed(parity, 0 if c < split else 1, half, c), c)
+        couple_parts = [
+            jnp.concatenate([couple[j, part_index] for j in range(n_fit)], axis=0)
+            for part_index in range(2)
+        ]
+        heights = virtual.shape[0]
 
         for t in range(0, active, 2):
             left = rows[:, t * lanes : (t + 1) * lanes]
             right = rows[:, (t + 1) * lanes : (t + 2) * lanes]
             plain = jnp.concatenate([left, right], axis=1)
             other = jnp.concatenate([turn(left, pairs), turn(right, pairs)], axis=1)
-            value = plain_product(couple_ref[0], plain) + plain_product(couple_ref[1], other)
-            virtual[:, t, :] = value[:, :lanes]
-            virtual[:, t + 1, :] = value[:, lanes:]
+            value = contract_first(couple_parts[0], plain) + contract_first(couple_parts[1], other)
+            virtual[:, t, :] = value[:heights, :lanes]
+            virtual[:, t + 1, :] = value[:heights, lanes:]
 
         for c in range(chunks):
             for side in range(2):
@@ -480,7 +518,6 @@
             whole_copy(k).wait_send()
 
         final = p == PASSES - 1
-        own = tile // active
 
         def back_chunk(c, carry):
             for k in range(n_fit):
@@ -548,16 +585,21 @@
     for c in range(chunks):
         gathered(c)
         back_sends(c)
+    for k in range(1, n_fit):
+        couple_copy(k).wait_send()
 
 
 FIRST_RELAYS = {1: 8, 2: 9, 3: 10, 5: 16, 6: 17, 7: 18, 9: 24, 10: 25, 11: 26}
 LATER_RELAYS = {0: 9, 3: 24, 4: 17, 6: 10, 7: 25, 8: 18, 10: 26}
 
 
-def all_passes(fit_rows, values, couple, src, den, act, active, n):
+def all_passes(fit_rows, source, give, eps, row, act, n):
     depth = fit_rows.shape[2]
-    chunks, n_fit, tile, lanes = values.shape
-    local_vir, wide = couple.shape[1:]
+    active, lanes = row.shape
+    n_fit, chunks = give.shape[0], CHUNKS
+    local_vir = eps.shape[0]
+    tile = local_vir // (chunks * n_fit) * active
+    wide = n_fit * give.shape[2]
     span = wide // (chunks * n)
     half = n // 2
     dma = pltpu.SemaphoreType.DMA
@@ -565,9 +607,10 @@
     each = pltpu.VMEM((chunks, tile, lanes), BF16)
     twice = pltpu.VMEM((chunks, 2, tile, lanes), BF16)
     state = pltpu.VMEM((chunks, tile, lanes), F32)
+    any_space = pl.BlockSpec(memory_space=pl.ANY)
     return pl.pallas_call(
         lambda *refs: passes_kernel(n, *refs),
-        in_specs=[pl.BlockSpec(memory_space=pl.ANY)] + whole_vmem(5),
+        in_specs=[any_space, any_space] + whole_vmem(4),
         out_specs=pl.BlockSpec(memory_space=pltpu.VMEM),
         out_shape=jax.ShapeDtypeStruct((chunks, n_fit, tile, lanes), BF16),
         scratch_shapes=[
@@ -589,18 +632,25 @@
             each,
             state,
             state,
+            state,
+            state,
+            state,
+            pltpu.VMEM((local_vir * active, lanes), F32),
+            pltpu.VMEM((tile, lanes), F32),
+            pltpu.VMEM(give.shape, BF16),
             dma((2, half, chunks)),
             dma((2, half, chunks)),
         ]
         + [dma((n - 1,))] * 4
         + [dma((2, chunks))]
+        + [dma((n_fit - 1,))] * 2
         + [dma((chunks, 2))] * 2
         + [dma((chunks,))] * 8,
         compiler_params=pltpu.CompilerParams(
             collective_id=0, has_side_effects=True, vmem_limit_bytes=60 * 2**20
         ),
         name="passes",
-    )(fit_rows, values, couple, src, den, act)
+    )(fit_rows, source, give, eps, row, act)
 
 
 def per_device(fitted, vcouple, actfock, eps_vir, eps_act, pair_energy, source):
@@ -613,26 +663,30 @@
     own = local_vir // (CHUNKS * n_fit)
     span = -(-own // 16) * 16
     held = block_rows // local_vir
+    high = -(-local_vir // 128) * 128
 
     row = eps_act[:, None] - pair_energy[None, :]
-    wide_row = jnp.concatenate([row, row], axis=1)
-    values, src, den = prologue(eps_vir, wide_row, source, n_fit)
-
-    couple = lax.dynamic_slice_in_dim(vcouple, vir_index * local_vir, local_vir, 2)
-    couple = couple.reshape(2, held, CHUNKS, n_fit, own, local_vir).transpose(3, 0, 1, 2, 4, 5)
-    couple = couple.reshape(n_fit, 2 * held * CHUNKS * own, local_vir)
-    couple = lax.all_to_all(couple, "fit", 0, 0)
-    couple = couple.reshape(n_fit, 2, held, CHUNKS, own, local_vir).transpose(1, 5, 3, 0, 2, 4)
-    couple = jnp.pad(couple, ((0, 0),) * 5 + ((0, span - own),))
-    couple = couple.reshape(2, local_vir, CHUNKS * n_vir * span)
+    row = jnp.concatenate([row, row], axis=1)
+    eps = jnp.broadcast_to(eps_vir[:, None], (local_vir, lanes))
+    flat = source.reshape(2, local_vir, active // 2, lanes)
+    flat = flat.transpose(1, 2, 0, 3).reshape(local_vir * active, lanes)
+
+    give = lax.dynamic_slice_in_dim(vcouple, vir_index * local_vir, local_vir, 2)
+    give = give.reshape(2, held, CHUNKS, n_fit, own, local_vir).transpose(3, 0, 1, 2, 4, 5)
+    give = jnp.pad(give, ((0, 0),) * 4 + ((0, span - own), (0, high - local_vir)))
+    give = give.reshape(n_fit, 2, held * CHUNKS * span, high)
 
     group = 5
     eye = jnp.eye(group, dtype=F32)
-    act = jnp.einsum("gh,cut->cgthu", eye, actfock).reshape(2, group * active, group * active)
+    act = jnp.einsum("gh,cut->gtchu", eye, actfock).reshape(group * active, 2 * group * active)
+    act_high = act.astype(BF16)
+    act_low = (act - act_high.astype(F32)).astype(BF16)
+    act = jnp.stack([act_high, act_low])
     fit_rows = fitted.reshape(2, local_vir * active, local_fit)
-    values = all_passes(fit_rows, values, couple, src, den, act, active, n_vir)
-    change = values.reshape(CHUNKS * n_fit, own * active, lanes)
-    return epilogue(eps_vir, row.reshape(1, active * pairs), source, change, active, lanes)
+    change = all_passes(fit_rows, flat, give, eps, row, act, n_vir)
+    out = epilogue(eps, row, flat, change.reshape(CHUNKS * n_fit, own * active, lanes))
+    out = out.reshape(local_vir, active // 2, 2, lanes).transpose(0, 2, 1, 3)
+    return out.reshape(local_vir, 2, active * pairs).transpose(1, 0, 2)
 
 
 def choose(mesh):

time: 287 us -> 271 us (0.944)
  Pallas kernels: 260 us -> 244 us
  starting transfers between devices: 4.24 us -> 0 us
    pallas_call x3 -> x2, Pallas kernels: 260 us -> 244 us  [the longest x1 237 us: all_passes(): pl.pallas_call(lambda *refs: passes_kernel(n, *refs), in_specs=[any_space...]
    transpose x1, local copies, waits for them, and re-layouts: 0.36 us -> 7.08 us  [per_device(): flat = flat.transpose(1, 2, 0, 3).reshape(local_vir * active, lanes)]
    pallas_call x1 -> x0, local copies, waits for them, and re-layouts: 4.69 us -> none  [epilogue(): pl.pallas_call(epilogue_kernel, in_specs=whole_vmem(4), out_specs=pl.Bloc...]
    all_to_all x1 -> x0, starting transfers between devices: 4.24 us -> none  [per_device(): couple = lax.all_to_all(couple, 'fit', 0, 0)]
    unnamed x23 -> x13, local copies, waits for them, and re-layouts: 9.53 us -> 6.39 us
  transfers between devices with their start and end apart: 1 -> 0, of which waited for: 0 -> 0; matrix products, arithmetic and copies ran while one was open for 1% -> 0% of each run, Pallas kernels for 2% -> 0%
where the time goes in v1:
time: 271 us; the launch traced here: 269 us
  Pallas kernels  244 us (90%)
  local copies, waits for them, and re-layouts  22.8 us (8%)
    pallas_call x1, Pallas kernels, all_passes(): pl.pallas_call(lambda *refs: passes_kernel(n, *refs), in_specs=[any_space...  237 us
    transpose x1, local copies, waits for them, and re-layouts, per_device(): flat = flat.transpose(1, 2, 0, 3).reshape(local_vir * active, lanes)  7.08 us
    pallas_call x1, Pallas kernels, epilogue(): pl.pallas_call(epilogue_kernel, grid=(pieces,), in_specs=[pl.BlockSpec(ep...  6.83 us
    unnamed x13, local copies, waits for them, and re-layouts  6.39 us

profile of v1, /device:TPU:0, one launch (start us, length us, event | category | flops | bytes accessed | tf_op | source)
XLA Modules:
  0.0 268.9 jit_solution(1500233966284978504)
XLA Ops:
  0.0 1.4 broadcast_in_dim.2.refs_3_.eps_ref
  1.4 0.7 broadcast_subtract_fusion
  2.2 0.7 pad_maximum_fusion.1.refs_4_.row_ref
  2.9 4.6 %copy.10 = f32[2,300,1536]{2,1,0:T(8,128)} copy(f32[2,300,1536]{2,0,1:T(2,128)} %param.13) | data formatting | bytes 7372800 | tf_op args[6]
  7.5 4.0 %reshape.59 = f32[2,300,12,128]{3,2,1,0:T(8,128)} reshape(f32[2,300,1536]{2,1,0:T(8,128)} %copy.10) | data formatting | bytes 7372800 | tf_op jit(solution)/shard_map/reshape | solution.py:671
  11.5 7.1 %copy.11 = f32[300,12,2,128]{3,2,1,0:T(2,128)} copy(f32[300,12,2,128]{3,1,0,2:T(8,128)} %bitcast.21) | data formatting | bytes 7372800 | tf_op jit(solution)/shard_map/transpose | solution.py:672
  18.6 0.0 copy-start.4
  18.6 1.7 constant_dynamic-slice_fusion
  20.3 0.7 copy.12
  21.0 0.2 copy.15
  21.2 1.2 pad.4.clone
  22.4 0.0 copy-done.4
  22.4 0.1 copy.14
  22.5 0.2 multiply_bitcast_fusion
  22.6 0.3 reshape.64
  22.9 0.7 pad_maximum_fusion.refs_5_
  23.6 0.0 copy-start
  23.6 236.9 %passes.1 = bf16[3,4,600,128]{3,2,1,0:T(8,128)(2,1)} custom-call(bf16[2,7200,1792]{2,1,0:T(8,128)(2,1)} %bitcast.20, f32[7200,128]{1,0:T(8,128)} %bitcast.17, bf16[4,2,192,384]{3,2,1,0:T(8,128)(2,1)} %bitcast.22, f32[300,128]{1,0:T(8,128)} %broadcast_in_dim.2.refs_3_.eps_ref, f32[24,128]{1,0:T(8,128)} %pad_maximum_fusion.1.refs_4_.row_ref, ...), custom_call_target="tpu_custom_call" | custom-call | tf_op jit(solution)/shard_map/passes/pallas_call | solution.py:611
  260.6 0.0 copy-done
  260.6 0.0 copy-done.2
  260.6 0.0 copy-done.3
  260.6 0.0 copy-start.1
  260.6 1.5 copy-done.1
  262.1 6.8 %epilogue.1 = f32[7200,128]{1,0:T(8,128)} custom-call(f32[300,128]{1,0:T(8,128)S(1)} %copy-done.2, f32[24,128]{1,0:T(8,128)S(1)} %copy-done.3, f32[7200,128]{1,0:T(8,128)S(1)} %bitcast.18, bf16[12,600,128]{2,1,0:T(8,128)(2,1)S(1)} %bitcast.19), custom_call_target="tpu_custom_call" | custom-call | tf_op jit(solution)/shard_map/epilogue/pallas_call | solution.py:116
  (4 shorter events, 0.0 us)
Async XLA Ops:
  18.6 3.8 %copy-start.4 = (f32[2,24,24]{2,1,0:T(8,128)S(1)}, f32[2,24,24]{2,1,0:T(8,128)}, u32[]{:S(2)}) copy-start(f32[2,24,24]{2,1,0:T(8,128)} %param.9) | copy-start | bytes 13828
  23.6 236.9 %copy-start = (f32[300,12,2,128]{3,2,1,0:T(2,128)S(1)}, f32[300,12,2,128]{3,2,1,0:T(2,128)}, u32[]{:S(2)}) copy-start(f32[300,12,2,128]{3,2,1,0:T(2,128)} %copy.11) | copy-start | bytes 11059204
  23.6 236.9 %copy-start.2 = (f32[300,128]{1,0:T(8,128)S(1)}, f32[300,128]{1,0:T(8,128)}, u32[]{:S(2)}) copy-start(f32[300,128]{1,0:T(8,128)} %broadcast_in_dim.2.refs_3_.eps_ref) | copy-start | bytes 460804
  23.6 237.0 %copy-start.3 = (f32[24,128]{1,0:T(8,128)S(1)}, f32[24,128]{1,0:T(8,128)}, u32[]{:S(2)}) copy-start(f32[24,128]{1,0:T(8,128)} %pad_maximum_fusion.1.refs_4_.row_ref) | copy-start | bytes 36868
  260.6 1.5 copy-start.1

commit v2 on v1

--- a/solution.py
+++ b/solution.py
@@ -1,13 +1,15 @@
 import jax
 import jax.numpy as jnp
 from jax import lax
+from jax.experimental.layout import Layout, with_layout_constraint
 from jax.experimental import pallas as pl
 from jax.experimental.pallas import tpu as pltpu
 from jax.sharding import PartitionSpec as P
 
 PASSES = 3
 CHUNKS = 3
-SLOTS = 3
+SLOTS = 6
+HALVES = 2
 BF16 = jnp.bfloat16
 F32 = jnp.float32
 MESH = pl.DeviceIdType.MESH
@@ -101,28 +103,34 @@
 
 
 def epilogue_kernel(eps_ref, row_ref, source_ref, change_ref, out_ref, den):
-    tile, lanes = source_ref.shape
+    group, tile, lanes = change_ref.shape
     active = row_ref.shape[0]
     own = tile // active
-    first = pl.program_id(0) * own
-    for i in range(own):
-        den[i * active : (i + 1) * active, :] = eps_ref[pl.ds(first + i, 1), :] + row_ref[...]
-    start = mix(source_ref[...], lanes // 2) / den[...]
-    out_ref[...] = mix(start + change_ref[0].astype(F32), lanes // 2)
+
+    def one(j, carry):
+        first = (pl.program_id(0) * group + j) * own
+        for i in range(own):
+            den[i * active : (i + 1) * active, :] = eps_ref[pl.ds(first + i, 1), :] + row_ref[...]
+        cut = pl.ds(pl.multiple_of(j * tile, 8), tile)
+        start = mix(source_ref[cut, :], lanes // 2) / den[...]
+        out_ref[cut, :] = mix(start + change_ref[j].astype(F32), lanes // 2)
+        return carry
+
+    lax.fori_loop(0, group, one, 0)
 
 
 def epilogue(eps, row, source, change):
     pieces, tile, lanes = change.shape
     return pl.pallas_call(
         epilogue_kernel,
-        grid=(pieces,),
+        grid=(pieces // CHUNKS,),
         in_specs=[
             pl.BlockSpec(eps.shape, lambda i: (0, 0)),
             pl.BlockSpec(row.shape, lambda i: (0, 0)),
-            pl.BlockSpec((tile, lanes), lambda i: (i, 0)),
-            pl.BlockSpec((1, tile, lanes), lambda i: (i, 0, 0)),
+            pl.BlockSpec((CHUNKS * tile, lanes), lambda i: (i, 0)),
+            pl.BlockSpec((CHUNKS, tile, lanes), lambda i: (i, 0, 0)),
         ],
-        out_specs=pl.BlockSpec((tile, lanes), lambda i: (i, 0)),
+        out_specs=pl.BlockSpec((CHUNKS * tile, lanes), lambda i: (i, 0)),
         out_shape=jax.ShapeDtypeStruct(source.shape, F32),
         scratch_shapes=[pltpu.VMEM((tile, lanes), F32)],
         compiler_params=pltpu.CompilerParams(vmem_limit_bytes=16 * 2**20),
@@ -161,7 +169,7 @@
     pairs = lanes // 2
     tiles = chunks * n_fit
     band = lanes // n
-    depth = acc.shape[1]
+    depth = acc.shape[2]
     active = virtual.shape[1]
     span = spread.shape[0] // active
     half = n // 2
@@ -174,10 +182,11 @@
     split = (chunks + 1) // 2
     group = act_ref.shape[1]
 
-    def fetch(row_tile, slot):
+    def fetch(row_tile, side, slot):
         row = pl.multiple_of(row_tile * tile, 8)
+        column = pl.multiple_of(side * depth, 128)
         return pltpu.make_async_copy(
-            f_ref.at[:, pl.ds(row, tile), :], buf.at[slot], buf_sem.at[slot]
+            f_ref.at[:, pl.ds(row, tile), pl.ds(column, depth)], buf.at[slot], buf_sem.at[slot]
         )
 
     def remote(src, dst, send, recv, axis, peer):
@@ -192,8 +201,16 @@
             value = value + jnp.where(k == j, order[j], 0)
         return value
 
+    def prefetch(g):
+        ahead = g + SLOTS - 1
+        phase = lax.rem(ahead // tiles, 2 * HALVES)
+        i = lax.rem(ahead, tiles)
+        k = lax.rem(i, n_fit)
+        which = jnp.where(phase == 2 * HALVES - 1, i - k + back_tile(k), i)
+        fetch(which, lax.rem(phase, HALVES), lax.rem(ahead, SLOTS)).start()
+
     for i in range(SLOTS - 1):
-        fetch(i, i).start()
+        fetch(i, 0, i).start()
     own = tile // active
     raw_copies = [
         pltpu.make_async_copy(
@@ -281,30 +298,51 @@
         for owner in owners:
             lay(parity, owner, c)
 
-    def part_copy(k):
+    def part_copy(h, k):
         peer = (vir + k) % n
         return remote(
-            part.at[peer], parts.at[vir], part_send.at[k - 1], part_recv.at[k - 1], "vir", peer
-        )
-
-    def part_landed(k):
+            part.at[h, peer], parts.at[h, vir], part_send.at[h, k - 1], part_recv.at[h, k - 1],
+            "vir", peer,
+        )
+
+    def part_landed(h, k):
         peer = (vir + n - k) % n
         remote(
-            part.at[peer], parts.at[peer], part_send.at[k - 1], part_recv.at[k - 1], "vir", peer
+            part.at[h, peer], parts.at[h, peer], part_send.at[h, k - 1], part_recv.at[h, k - 1],
+            "vir", peer,
         ).wait_recv()
         return peer
 
-    def whole_copy(k):
+    def whole_copy(h, k):
         peer = (vir + k) % n
-        return remote(
-            whole.at[vir], whole.at[vir], whole_send.at[k - 1], whole_recv.at[k - 1], "vir", peer
-        )
-
-    def whole_landed(k):
+        slot = whole.at[h, vir]
+        return remote(slot, slot, whole_send.at[h, k - 1], whole_recv.at[h, k - 1], "vir", peer)
+
+    def whole_landed(h, k):
         peer = (vir + n - k) % n
-        remote(
-            whole.at[peer], whole.at[peer], whole_send.at[k - 1], whole_recv.at[k - 1], "vir", peer
-        ).wait_recv()
+        slot = whole.at[h, peer]
+        remote(slot, slot, whole_send.at[h, k - 1], whole_recv.at[h, k - 1], "vir", peer).wait_recv()
+
+    def give_parts(h):
+        for k in range(n):
+            part[h, k] = acc[h, k * band : (k + 1) * band, :].astype(BF16)
+        for k in range(1, n):
+            part_copy(h, k).start()
+
+    def sum_parts(h):
+        total = acc[h, pl.ds(pl.multiple_of(vir * band, band), band), :]
+        for k in range(1, n):
+            total = total + parts[h, part_landed(h, k)].astype(F32)
+        whole[h, vir] = total.astype(BF16)
+        for k in range(1, n):
+            whole_copy(h, k).start()
+
+    def take_whole(h):
+        for k in range(1, n):
+            whole_landed(h, k)
+        cols = whole[h].reshape(lanes, depth).astype(F32).T
+        inter[h] = cols.astype(BF16)
+        turned[h] = turn(cols, pairs).astype(BF16)
 
     def near_copy(c, k):
         return remote(
@@ -415,49 +453,59 @@
         later = p > 0
         acc[...] = jnp.zeros_like(acc)
 
-        def contract_step(i, carry):
-            ahead = i + SLOTS - 1
-            inside = ahead < tiles
-            target = jnp.where(inside, ahead, back_tile(ahead - tiles))
-            fetch(target, lax.rem(ahead, SLOTS)).start()
+        def scheduled(g):
+            code = jnp.where(later, choose_int(g, LATER_RELAYS), choose_int(g, FIRST_RELAYS))
+
+            @pl.when(code > 0)
+            def _():
+                relay(parity, code // 8, lax.rem(code, 8))
+
+        @pl.when(later)
+        def _():
+            update(last_chunk - 1, parity, False)
+            pass_on(0)
+
+        def contract_step(g, carry):
+            prefetch(g)
+            h = g // tiles
+            i = lax.rem(g, tiles)
             c = i // n_fit
             j = lax.rem(i, n_fit)
 
-            @pl.when(later & (j == 0))
+            @pl.when(later & (h == 0) & (j == 0))
             def _():
                 gathered(c)
 
-            slot = lax.rem(i, SLOTS)
-            fetch(i, slot).wait()
+            slot = lax.rem(g, SLOTS)
+            fetch(i, h, slot).wait()
             values = x_ref[c, j]
-            acc[...] += lax.dot_general(
+            acc[h] += lax.dot_general(
                 values, buf[slot, 0], contract, preferred_element_type=F32
             ) + lax.dot_general(
                 -turn(values, pairs), buf[slot, 1], contract, preferred_element_type=F32
             )
 
-            @pl.when(later & (i == 2))
+            @pl.when(later & (g == 0))
             def _():
                 update(last_chunk, parity, False)
 
-            @pl.when(later & ((i == 1) | (i == 5)))
+            @pl.when(later & ((g == 2) | (g == 6)))
             def _():
-                pass_on(jnp.where(i == 1, last_chunk - 1, last_chunk))
-
-            code = jnp.where(later, choose_int(i, LATER_RELAYS), choose_int(i, FIRST_RELAYS))
-
-            @pl.when(code > 0)
+                pass_on(jnp.where(g == 2, last_chunk - 1, last_chunk))
+
+            @pl.when(g == tiles - 1)
             def _():
-                relay(parity, code // 8, lax.rem(code, 8))
-
+                give_parts(0)
+
+            @pl.when(g == FIRST_SUM)
+            def _():
+                sum_parts(0)
+
+            scheduled(g)
             return carry
 
-        lax.fori_loop(0, tiles, contract_step, 0)
-
-        for k in range(n):
-            part[k] = acc[k * band : (k + 1) * band, :].astype(BF16)
-        for k in range(1, n):
-            part_copy(k).start()
+        lax.fori_loop(0, HALVES * tiles, contract_step, 0)
+        give_parts(1)
 
         @pl.when(later)
         def _():
@@ -474,12 +522,24 @@
             for k in range(1, n_fit):
                 couple_landed(k)
 
-        total = acc[pl.ds(pl.multiple_of(vir * band, band), band), :]
-        for k in range(1, n):
-            total = total + parts[part_landed(k)].astype(F32)
-        whole[vir] = total.astype(BF16)
-        for k in range(1, n):
-            whole_copy(k).start()
+        take_whole(0)
+
+        def first_back(i, carry):
+            g = HALVES * tiles + i
+            prefetch(g)
+            slot = lax.rem(g, SLOTS)
+            fetch(i, 0, slot).wait()
+            value = plain_product(buf[slot, 0], inter[0]) + plain_product(buf[slot, 1], turned[0])
+            virtual[pl.ds(i * own, own)] = value.reshape(own, active, lanes)
+
+            @pl.when(i == SECOND_SUM)
+            def _():
+                sum_parts(1)
+
+            scheduled(g)
+            return carry
+
+        lax.fori_loop(0, tiles, first_back, 0)
         for c in range(chunks):
             lay(parity, landed(parity, 0 if c < split else 1, half, c), c)
         couple_parts = [
@@ -494,51 +554,37 @@
             plain = jnp.concatenate([left, right], axis=1)
             other = jnp.concatenate([turn(left, pairs), turn(right, pairs)], axis=1)
             value = contract_first(couple_parts[0], plain) + contract_first(couple_parts[1], other)
-            virtual[:, t, :] = value[:heights, :lanes]
-            virtual[:, t + 1, :] = value[:heights, lanes:]
+            virtual[:, t, :] += value[:heights, :lanes]
+            virtual[:, t + 1, :] += value[:heights, lanes:]
 
         for c in range(chunks):
             for side in range(2):
                 for stage in range(1, half + 1):
                     if stage < half or sent_last(side, c):
                         hop(parity, side, stage, c).wait_send()
-        for k in range(1, n):
-            whole_landed(k)
-        block = depth
-        for width in (512, 384, 256, 128):
-            if depth % width == 0:
-                block = width
-                break
-        for q in range(0, depth, block):
-            cols = whole[:, :, q : q + block].reshape(lanes, block).astype(F32).T
-            inter[q : q + block, :] = cols.astype(BF16)
-            turned[q : q + block, :] = turn(cols, pairs).astype(BF16)
-        for k in range(1, n):
-            part_copy(k).wait_send()
-            whole_copy(k).wait_send()
+        take_whole(1)
+        for h in range(HALVES):
+            for k in range(1, n):
+                part_copy(h, k).wait_send()
+                whole_copy(h, k).wait_send()
 
         final = p == PASSES - 1
 
         def back_chunk(c, carry):
             for k in range(n_fit):
                 i = c * n_fit + k
-                ahead = i + SLOTS - 1
-                inside = ahead < tiles
-                after = ahead - tiles
-                target = jnp.where(
-                    inside, (ahead // n_fit) * n_fit + order[(k + SLOTS - 1) % n_fit], after
-                )
-
-                @pl.when(inside | jnp.logical_not(final))
+                g = (HALVES + 1) * tiles + i
+
+                @pl.when((i + SLOTS - 1 < tiles) | jnp.logical_not(final))
                 def _():
-                    fetch(target, lax.rem(ahead, SLOTS)).start()
-
-                slot = lax.rem(i, SLOTS)
+                    prefetch(g)
+
+                slot = lax.rem(g, SLOTS)
                 where = c * n_fit + order[k]
-                fetch(where, slot).wait()
+                fetch(where, 1, slot).wait()
                 value = (
-                    plain_product(buf[slot, 0], inter[...])
-                    + plain_product(buf[slot, 1], turned[...])
+                    plain_product(buf[slot, 0], inter[1])
+                    + plain_product(buf[slot, 1], turned[1])
                     + virtual[pl.ds(where * own, own)].reshape(tile, lanes)
                 )
                 if k < 2:
@@ -553,25 +599,9 @@
                     kept[c] = value + near_in[c, 1].astype(F32)
                 if k == 0:
 
-                    @pl.when(c >= 2)
+                    @pl.when(c == 2)
                     def _():
-                        pass_on(c - 2)
-
-                    @pl.when((c >= 2) & jnp.logical_not(final))
-                    def _():
-                        relay(1 - parity, 1, c - 2)
-
-                if k == 1:
-
-                    @pl.when(c >= 1)
-                    def _():
-                        update(c - 1, 1 - parity, final)
-
-                if k == 3:
-
-                    @pl.when((c >= 2) & jnp.logical_not(final))
-                    def _():
-                        relay(1 - parity, 2, c - 2)
+                        update(0, 1 - parity, final)
 
             return carry
 
@@ -579,8 +609,10 @@
         return carry
 
     lax.fori_loop(0, PASSES, one_pass, 0)
+    update(last_chunk - 1, 0, True)
+    pass_on(0)
+    update(last_chunk, 0, True)
     pass_on(last_chunk - 1)
-    update(last_chunk, 0, True)
     pass_on(last_chunk)
     for c in range(chunks):
         gathered(c)
@@ -589,12 +621,14 @@
         couple_copy(k).wait_send()
 
 
-FIRST_RELAYS = {1: 8, 2: 9, 3: 10, 5: 16, 6: 17, 7: 18, 9: 24, 10: 25, 11: 26}
-LATER_RELAYS = {0: 9, 3: 24, 4: 17, 6: 10, 7: 25, 8: 18, 10: 26}
+FIRST_RELAYS = {5: 8, 9: 9, 13: 10, 17: 16, 20: 17, 23: 18, 27: 24, 30: 25, 33: 26}
+LATER_RELAYS = {1: 8, 3: 9, 7: 16, 9: 10, 12: 17, 16: 24, 20: 18, 24: 25, 28: 26}
+FIRST_SUM = 20
+SECOND_SUM = 6
 
 
 def all_passes(fit_rows, source, give, eps, row, act, n):
-    depth = fit_rows.shape[2]
+    depth = fit_rows.shape[2] // HALVES
     active, lanes = row.shape
     n_fit, chunks = give.shape[0], CHUNKS
     local_vir = eps.shape[0]
@@ -603,7 +637,7 @@
     span = wide // (chunks * n)
     half = n // 2
     dma = pltpu.SemaphoreType.DMA
-    band = pltpu.VMEM((n, lanes // n, depth), BF16)
+    band = pltpu.VMEM((HALVES, n, lanes // n, depth), BF16)
     each = pltpu.VMEM((chunks, tile, lanes), BF16)
     twice = pltpu.VMEM((chunks, 2, tile, lanes), BF16)
     state = pltpu.VMEM((chunks, tile, lanes), F32)
@@ -616,12 +650,12 @@
         scratch_shapes=[
             pltpu.VMEM((SLOTS, 2, tile, depth), BF16),
             dma((SLOTS,)),
-            pltpu.VMEM((lanes, depth), F32),
+            pltpu.VMEM((HALVES, lanes, depth), F32),
             band,
             band,
             band,
-            pltpu.VMEM((depth, lanes), BF16),
-            pltpu.VMEM((depth, lanes), BF16),
+            pltpu.VMEM((HALVES, depth, lanes), BF16),
+            pltpu.VMEM((HALVES, depth, lanes), BF16),
             pltpu.VMEM((2, n, chunks, tile, lanes), BF16),
             pltpu.VMEM((span * active, lanes), F32),
             pltpu.VMEM((wide, active * lanes), BF16),
@@ -641,7 +675,7 @@
             dma((2, half, chunks)),
             dma((2, half, chunks)),
         ]
-        + [dma((n - 1,))] * 4
+        + [dma((HALVES, n - 1))] * 4
         + [dma((2, chunks))]
         + [dma((n_fit - 1,))] * 2
         + [dma((chunks, 2))] * 2
@@ -669,6 +703,7 @@
     row = jnp.concatenate([row, row], axis=1)
     eps = jnp.broadcast_to(eps_vir[:, None], (local_vir, lanes))
     flat = source.reshape(2, local_vir, active // 2, lanes)
+    flat = with_layout_constraint(flat, Layout(major_to_minor=(1, 2, 0, 3)))
     flat = flat.transpose(1, 2, 0, 3).reshape(local_vir * active, lanes)
 
     give = lax.dynamic_slice_in_dim(vcouple, vir_index * local_vir, local_vir, 2)
@@ -679,9 +714,8 @@
     group = 5
     eye = jnp.eye(group, dtype=F32)
     act = jnp.einsum("gh,cut->gtchu", eye, actfock).reshape(group * active, 2 * group * active)
-    act_high = act.astype(BF16)
-    act_low = (act - act_high.astype(F32)).astype(BF16)
-    act = jnp.stack([act_high, act_low])
+    act_high = lax.reduce_precision(act, 8, 7)
+    act = jnp.stack([act_high, act - act_high]).astype(BF16)
     fit_rows = fitted.reshape(2, local_vir * active, local_fit)
     change = all_passes(fit_rows, flat, give, eps, row, act, n_vir)
     out = epilogue(eps, row, flat, change.reshape(CHUNKS * n_fit, own * active, lanes))
@@ -704,7 +738,7 @@
             and local_vir % (CHUNKS * n_fit * 5) == 0
             and vcouple.shape[1] % local_vir == 0
             and active % 8 == 0
-            and local_fit % 128 == 0
+            and local_fit % (128 * HALVES) == 0
         )
         return per_device(*args) if fits else plain_device(*args)
 

time: 271 us -> 264 us (0.974)
  local copies, waits for them, and re-layouts: 22.8 us -> 7.83 us
  Pallas kernels: 244 us -> 253 us
    pallas_call x1, Pallas kernels: 237 us -> 248 us  [all_passes(): pl.pallas_call(lambda *refs: passes_kernel(n, *refs), in_specs=[any_space...]
    transpose x1 -> x0, local copies, waits for them, and re-layouts: 7.08 us -> none  [per_device(): flat = flat.transpose(1, 2, 0, 3).reshape(local_vir * active, lanes)]
    reshape x1 -> x0, local copies, waits for them, and re-layouts: 4.04 us -> none  [per_device(): flat = source.reshape(2, local_vir, active // 2, lanes)]
    unnamed x13 -> x10, local copies, waits for them, and re-layouts: 6.39 us -> 2.52 us
where the time goes in v2:
time: 264 us; the launch traced here: 263 us
  Pallas kernels  253 us (96%)
  local copies, waits for them, and re-layouts  7.83 us (3%)
    pallas_call x1, Pallas kernels, all_passes(): pl.pallas_call(lambda *refs: passes_kernel(n, *refs), in_specs=[any_space...  248 us

profile of v2, /device:TPU:0, one launch (start us, length us, event | category | flops | bytes accessed | tf_op | source)
XLA Modules:
  0.0 263.3 jit_solution(14665297891749116112)
XLA Ops:
  0.0 0.7 broadcast_subtract_fusion
  0.7 0.7 pad_maximum_fusion.1.refs_4_.row_ref
  1.4 0.8 copy.11
  2.2 1.5 broadcast_in_dim.2.refs_3_.eps_ref
  3.7 1.7 constant_dynamic-slice_fusion
  5.4 0.7 copy.9
  6.1 0.2 copy.12
  6.3 1.2 pad.4.clone
  7.5 0.1 multiply_bitcast_fusion
  7.6 0.3 reshape.58
  7.9 0.7 pad_maximum_fusion.refs_5_
  8.6 0.0 copy-start
  8.6 0.0 copy-start.2
  8.6 0.0 copy-start.3
  8.6 247.9 %passes.1 = bf16[3,4,600,128]{3,2,1,0:T(8,128)(2,1)} custom-call(bf16[2,7200,1792]{2,1,0:T(8,128)(2,1)} %bitcast.23, f32[7200,128]{1,0:T(8,128)} %bitcast.20, bf16[4,2,192,384]{3,2,1,0:T(8,128)(2,1)} %bitcast.24, f32[300,128]{1,0:T(8,128)} %broadcast_in_dim.2.refs_3_.eps_ref, f32[24,128]{1,0:T(8,128)} %pad_maximum_fusion.1.refs_4_.row_ref, ...), custom_call_target="tpu_custom_call" | custom-call | tf_op jit(solution)/shard_map/passes/pallas_call | solution.py:645
  256.5 0.0 copy-done
  256.5 0.0 copy-done.2
  256.5 0.0 copy-done.3
  256.5 0.0 copy-start.1
  256.5 1.5 copy-done.1
  258.0 5.2 %epilogue.1 = f32[7200,128]{1,0:T(8,128)} custom-call(f32[300,128]{1,0:T(8,128)S(1)} %copy-done.2, f32[24,128]{1,0:T(8,128)S(1)} %copy-done.3, f32[7200,128]{1,0:T(8,128)S(1)} %bitcast.21, bf16[12,600,128]{2,1,0:T(8,128)(2,1)S(1)} %bitcast.22), custom_call_target="tpu_custom_call" | custom-call | tf_op jit(solution)/shard_map/epilogue/pallas_call | solution.py:124
  (2 shorter events, 0.0 us)
Async XLA Ops:
  8.6 247.9 %copy-start = (f32[2,300,1536]{2,0,1:T(2,128)S(1)}, f32[2,300,1536]{2,0,1:T(2,128)}, u32[]{:S(2)}) copy-start(f32[2,300,1536]{2,0,1:T(2,128)} %param.13) | copy-start | bytes 11059204
  8.6 247.9 %copy-start.2 = (f32[300,128]{1,0:T(8,128)S(1)}, f32[300,128]{1,0:T(8,128)}, u32[]{:S(2)}) copy-start(f32[300,128]{1,0:T(8,128)} %broadcast_in_dim.2.refs_3_.eps_ref) | copy-start | bytes 460804
  8.6 247.9 %copy-start.3 = (f32[24,128]{1,0:T(8,128)S(1)}, f32[24,128]{1,0:T(8,128)}, u32[]{:S(2)}) copy-start(f32[24,128]{1,0:T(8,128)} %pad_maximum_fusion.1.refs_4_.row_ref) | copy-start | bytes 36868
  256.5 1.5 copy-start.1

commit v3 on v1

--- a/solution.py
+++ b/solution.py
@@ -1,6 +1,7 @@
 import jax
 import jax.numpy as jnp
 from jax import lax
+from jax.experimental.layout import Layout, with_layout_constraint
 from jax.experimental import pallas as pl
 from jax.experimental.pallas import tpu as pltpu
 from jax.sharding import PartitionSpec as P
@@ -101,28 +102,34 @@
 
 
 def epilogue_kernel(eps_ref, row_ref, source_ref, change_ref, out_ref, den):
-    tile, lanes = source_ref.shape
+    group, tile, lanes = change_ref.shape
     active = row_ref.shape[0]
     own = tile // active
-    first = pl.program_id(0) * own
-    for i in range(own):
-        den[i * active : (i + 1) * active, :] = eps_ref[pl.ds(first + i, 1), :] + row_ref[...]
-    start = mix(source_ref[...], lanes // 2) / den[...]
-    out_ref[...] = mix(start + change_ref[0].astype(F32), lanes // 2)
+
+    def one(j, carry):
+        first = (pl.program_id(0) * group + j) * own
+        for i in range(own):
+            den[i * active : (i + 1) * active, :] = eps_ref[first + i] + row_ref[...]
+        cut = pl.ds(pl.multiple_of(j * tile, 8), tile)
+        start = mix(source_ref[cut, :], lanes // 2) / den[...]
+        out_ref[cut, :] = mix(start + change_ref[j].astype(F32), lanes // 2)
+        return carry
+
+    lax.fori_loop(0, group, one, 0)
 
 
 def epilogue(eps, row, source, change):
     pieces, tile, lanes = change.shape
     return pl.pallas_call(
         epilogue_kernel,
-        grid=(pieces,),
+        grid=(pieces // CHUNKS,),
         in_specs=[
-            pl.BlockSpec(eps.shape, lambda i: (0, 0)),
+            pl.BlockSpec(memory_space=pltpu.SMEM),
             pl.BlockSpec(row.shape, lambda i: (0, 0)),
-            pl.BlockSpec((tile, lanes), lambda i: (i, 0)),
-            pl.BlockSpec((1, tile, lanes), lambda i: (i, 0, 0)),
+            pl.BlockSpec((CHUNKS * tile, lanes), lambda i: (i, 0)),
+            pl.BlockSpec((CHUNKS, tile, lanes), lambda i: (i, 0, 0)),
         ],
-        out_specs=pl.BlockSpec((tile, lanes), lambda i: (i, 0)),
+        out_specs=pl.BlockSpec((CHUNKS * tile, lanes), lambda i: (i, 0)),
         out_shape=jax.ShapeDtypeStruct(source.shape, F32),
         scratch_shapes=[pltpu.VMEM((tile, lanes), F32)],
         compiler_params=pltpu.CompilerParams(vmem_limit_bytes=16 * 2**20),
@@ -151,7 +158,7 @@
 def passes_kernel(
     n, f_ref, source_ref, give_ref, eps_ref, row_ref, act_ref, x_ref,
     buf, buf_sem, acc, part, parts, whole, inter, turned, ring, spread, rows, virtual,
-    near, near_in, far, far_in, kept, amp, src, inverse, base, raw, den, couple,
+    near, near_in, far, far_in, kept, amp, src, inverse, base, raw, den, couple, flipped,
     ring_send, ring_recv, part_send, part_recv, whole_send, whole_recv, init_sem,
     couple_send, couple_recv,
     near_send, near_recv, far_send, far_recv, gx_send, gx_recv, gc_send, gc_recv, gr_send, gr_recv,
@@ -219,7 +226,7 @@
 
     def fill(first):
         for i in range(own):
-            den[i * active : (i + 1) * active, :] = eps_ref[pl.ds(first + i, 1), :] + row_ref[...]
+            den[i * active : (i + 1) * active, :] = eps_ref[first + i] + row_ref[...]
 
     def begin(c, carry):
         fill((c * n_fit + fit) * own)
@@ -473,6 +480,12 @@
             own_couple.wait()
             for k in range(1, n_fit):
                 couple_landed(k)
+            deep = couple.shape[2]
+            for side in range(2):
+                for j in range(n_fit):
+                    flipped[side, :, j * deep : (j + 1) * deep] = (
+                        couple[j, side].astype(F32).T.astype(BF16)
+                    )
 
         total = acc[pl.ds(pl.multiple_of(vir * band, band), band), :]
         for k in range(1, n):
@@ -482,18 +495,17 @@
             whole_copy(k).start()
         for c in range(chunks):
             lay(parity, landed(parity, 0 if c < split else 1, half, c), c)
-        couple_parts = [
-            jnp.concatenate([couple[j, part_index] for j in range(n_fit)], axis=0)
-            for part_index in range(2)
-        ]
         heights = virtual.shape[0]
+        padded = -(-heights // 16) * 16
 
         for t in range(0, active, 2):
             left = rows[:, t * lanes : (t + 1) * lanes]
             right = rows[:, (t + 1) * lanes : (t + 2) * lanes]
             plain = jnp.concatenate([left, right], axis=1)
             other = jnp.concatenate([turn(left, pairs), turn(right, pairs)], axis=1)
-            value = contract_first(couple_parts[0], plain) + contract_first(couple_parts[1], other)
+            value = plain_product(flipped[0, :padded], plain) + plain_product(
+                flipped[1, :padded], other
+            )
             virtual[:, t, :] = value[:heights, :lanes]
             virtual[:, t + 1, :] = value[:heights, lanes:]
 
@@ -610,7 +622,10 @@
     any_space = pl.BlockSpec(memory_space=pl.ANY)
     return pl.pallas_call(
         lambda *refs: passes_kernel(n, *refs),
-        in_specs=[any_space, any_space] + whole_vmem(4),
+        in_specs=[any_space, any_space]
+        + whole_vmem(1)
+        + [pl.BlockSpec(memory_space=pltpu.SMEM)]
+        + whole_vmem(2),
         out_specs=pl.BlockSpec(memory_space=pltpu.VMEM),
         out_shape=jax.ShapeDtypeStruct((chunks, n_fit, tile, lanes), BF16),
         scratch_shapes=[
@@ -638,6 +653,7 @@
             pltpu.VMEM((local_vir * active, lanes), F32),
             pltpu.VMEM((tile, lanes), F32),
             pltpu.VMEM(give.shape, BF16),
+            pltpu.VMEM((2, give.shape[3], wide), BF16),
             dma((2, half, chunks)),
             dma((2, half, chunks)),
         ]
@@ -667,8 +683,8 @@
 
     row = eps_act[:, None] - pair_energy[None, :]
     row = jnp.concatenate([row, row], axis=1)
-    eps = jnp.broadcast_to(eps_vir[:, None], (local_vir, lanes))
     flat = source.reshape(2, local_vir, active // 2, lanes)
+    flat = with_layout_constraint(flat, Layout(major_to_minor=(1, 2, 0, 3)))
     flat = flat.transpose(1, 2, 0, 3).reshape(local_vir * active, lanes)
 
     give = lax.dynamic_slice_in_dim(vcouple, vir_index * local_vir, local_vir, 2)
@@ -679,12 +695,11 @@
     group = 5
     eye = jnp.eye(group, dtype=F32)
     act = jnp.einsum("gh,cut->gtchu", eye, actfock).reshape(group * active, 2 * group * active)
-    act_high = act.astype(BF16)
-    act_low = (act - act_high.astype(F32)).astype(BF16)
-    act = jnp.stack([act_high, act_low])
+    act_high = lax.reduce_precision(act, 8, 7)
+    act = jnp.stack([act_high, act - act_high]).astype(BF16)
     fit_rows = fitted.reshape(2, local_vir * active, local_fit)
-    change = all_passes(fit_rows, flat, give, eps, row, act, n_vir)
-    out = epilogue(eps, row, flat, change.reshape(CHUNKS * n_fit, own * active, lanes))
+    change = all_passes(fit_rows, flat, give, eps_vir, row, act, n_vir)
+    out = epilogue(eps_vir, row, flat, change.reshape(CHUNKS * n_fit, own * active, lanes))
     out = out.reshape(local_vir, active // 2, 2, lanes).transpose(0, 2, 1, 3)
     return out.reshape(local_vir, 2, active * pairs).transpose(1, 0, 2)
 

time: 271 us -> 254 us (0.937)
  local copies, waits for them, and re-layouts: 22.8 us -> 6.37 us
    transpose x1 -> x0, local copies, waits for them, and re-layouts: 7.08 us -> none  [per_device(): flat = flat.transpose(1, 2, 0, 3).reshape(local_vir * active, lanes)]
    reshape x1 -> x0, local copies, waits for them, and re-layouts: 4.04 us -> none  [per_device(): flat = source.reshape(2, local_vir, active // 2, lanes)]
    unnamed x13 -> x10, local copies, waits for them, and re-layouts: 6.39 us -> 2.52 us
where the time goes in v3:
time: 254 us
  Pallas kernels  245 us (96%)
  local copies, waits for them, and re-layouts  6.37 us (3%)
    pallas_call x1, Pallas kernels, all_passes(): pl.pallas_call(lambda *refs: passes_kernel(n, *refs), in_specs=[any_space...  240 us
    pallas_call x1, Pallas kernels, epilogue(): pl.pallas_call(epilogue_kernel, grid=(pieces // CHUNKS,), in_specs=[pl.Bl...  5.8 us

profile of v3, /device:TPU:0, one launch (start us, length us, event | category | flops | bytes accessed | tf_op | source)
XLA Modules:
  0.0 254.1 jit_solution(3200848390811676209)
XLA Ops:
  0.0 0.7 broadcast_subtract_fusion
  0.7 0.7 pad_maximum_fusion.1.refs_4_.row_ref
  1.4 0.8 copy.11
  2.2 1.7 constant_dynamic-slice_fusion
  3.9 0.7 copy.9
  4.6 0.2 copy.12
  4.8 1.2 pad.4.clone
  6.0 0.1 multiply_bitcast_fusion
  6.2 0.3 reshape.57
  6.5 0.7 pad_maximum_fusion.refs_5_
  7.2 0.0 copy-start
  7.2 0.0 copy-start.2
  7.2 0.0 copy-start.3
  7.2 239.6 %passes.1 = bf16[3,4,600,128]{3,2,1,0:T(8,128)(2,1)} custom-call(bf16[2,7200,1792]{2,1,0:T(8,128)(2,1)} %bitcast.23, f32[7200,128]{1,0:T(8,128)} %bitcast.20, bf16[4,2,192,384]{3,2,1,0:T(8,128)(2,1)} %bitcast.24, f32[300]{0:T(512)} %eps_ref.1, f32[24,128]{1,0:T(8,128)} %pad_maximum_fusion.1.refs_4_.row_ref, bf16[2,120,240]{2,1,0:T(8,128)(2,1)} %pad_maximum_fusion.refs_5_), custom_call_target="tpu_custom_call" | custom-call | tf_op jit(solution)/shard_map/passes/pallas_call | solution.py:623
  246.7 0.0 copy-done
  246.8 0.0 copy-done.2
  246.8 0.0 copy-done.3
  246.8 0.0 copy-start.1
  246.8 1.5 copy-done.1
  248.3 5.8 %epilogue.1 = f32[7200,128]{1,0:T(8,128)} custom-call(f32[300]{0:T(512)S(1)} %copy-done.3, f32[24,128]{1,0:T(8,128)S(1)} %copy-done.2, f32[7200,128]{1,0:T(8,128)S(1)} %bitcast.21, bf16[12,600,128]{2,1,0:T(8,128)(2,1)S(1)} %bitcast.22), custom_call_target="tpu_custom_call" | custom-call | tf_op jit(solution)/shard_map/epilogue/pallas_call | solution.py:123
  (2 shorter events, 0.0 us)
Async XLA Ops:
  7.2 239.6 %copy-start = (f32[2,300,1536]{2,0,1:T(2,128)S(1)}, f32[2,300,1536]{2,0,1:T(2,128)}, u32[]{:S(2)}) copy-start(f32[2,300,1536]{2,0,1:T(2,128)} %param.13) | copy-start | bytes 11059204
  7.2 239.6 %copy-start.2 = (f32[24,128]{1,0:T(8,128)S(1)}, f32[24,128]{1,0:T(8,128)}, u32[]{:S(2)}) copy-start(f32[24,128]{1,0:T(8,128)} %pad_maximum_fusion.1.refs_4_.row_ref) | copy-start | bytes 36868
  7.2 239.6 %copy-start.3 = (f32[300]{0:T(512)S(1)}, f32[300]{0:T(512)}, u32[]{:S(2)}) copy-start(f32[300]{0:T(512)} %eps_ref.1) | copy-start | bytes 3604
  246.8 1.5 copy-start.1

commit v4 on v3

--- a/solution.py
+++ b/solution.py
@@ -157,9 +157,10 @@
 
 def passes_kernel(
     n, f_ref, source_ref, give_ref, eps_ref, row_ref, act_ref, x_ref,
-    buf, buf_sem, acc, part, parts, whole, inter, turned, ring, spread, rows, virtual,
+    buf, buf_sem, acc, part, side_in, line, line_in, whole, inter, turned, ring, spread, rows, virtual,
     near, near_in, far, far_in, kept, amp, src, inverse, base, raw, den, couple, flipped,
-    ring_send, ring_recv, part_send, part_recv, whole_send, whole_recv, init_sem,
+    ring_send, ring_recv, side_send, side_recv, line_send, line_recv, whole_send, whole_recv,
+    pass_send, pass_recv, init_sem,
     couple_send, couple_recv,
     near_send, near_recv, far_send, far_recv, gx_send, gx_recv, gc_send, gc_recv, gr_send, gr_recv,
 ):
@@ -169,6 +170,9 @@
     tiles = chunks * n_fit
     band = lanes // n
     depth = acc.shape[1]
+    line_size = n // 2
+    level, lane_side = vir // 2, vir % 2
+    partner = vir + 1 - 2 * lane_side
     active = virtual.shape[1]
     span = spread.shape[0] // active
     half = n // 2
@@ -288,30 +292,42 @@
         for owner in owners:
             lay(parity, owner, c)
 
-    def part_copy(k):
-        peer = (vir + k) % n
+    def side_copy():
         return remote(
-            part.at[peer], parts.at[vir], part_send.at[k - 1], part_recv.at[k - 1], "vir", peer
-        )
-
-    def part_landed(k):
-        peer = (vir + n - k) % n
+            part.at[1 - lane_side], side_in, side_send.at[0], side_recv.at[0], "vir", partner
+        )
+
+    def line_copy(k):
+        to = (level + k) % line_size
+        return remote(
+            line.at[to], line_in.at[level], line_send.at[k - 1], line_recv.at[k - 1],
+            "vir", 2 * to + lane_side,
+        )
+
+    def line_landed(k):
+        source = (level + line_size - k) % line_size
         remote(
-            part.at[peer], parts.at[peer], part_send.at[k - 1], part_recv.at[k - 1], "vir", peer
+            line.at[source], line_in.at[source], line_send.at[k - 1], line_recv.at[k - 1],
+            "vir", 2 * source + lane_side,
         ).wait_recv()
-        return peer
+        return source
 
     def whole_copy(k):
-        peer = (vir + k) % n
-        return remote(
-            whole.at[vir], whole.at[vir], whole_send.at[k - 1], whole_recv.at[k - 1], "vir", peer
-        )
+        slot = whole.at[vir]
+        peer = partner if k == 0 else 2 * ((level + k) % line_size) + lane_side
+        return remote(slot, slot, whole_send.at[k], whole_recv.at[k], "vir", peer)
 
     def whole_landed(k):
-        peer = (vir + n - k) % n
-        remote(
-            whole.at[peer], whole.at[peer], whole_send.at[k - 1], whole_recv.at[k - 1], "vir", peer
-        ).wait_recv()
+        peer = partner if k == 0 else 2 * ((level + line_size - k) % line_size) + lane_side
+        slot = whole.at[peer]
+        remote(slot, slot, whole_send.at[k], whole_recv.at[k], "vir", peer).wait_recv()
+
+    def pass_copy(k, side):
+        slot = whole.at[2 * ((level + line_size - k) % line_size) + side]
+        return remote(slot, slot, pass_send.at[k - 1], pass_recv.at[k - 1], "vir", partner)
+
+    def own_band(index):
+        return pl.ds(pl.multiple_of((2 * index + lane_side) * band, band), band)
 
     def near_copy(c, k):
         return remote(
@@ -462,9 +478,8 @@
         lax.fori_loop(0, tiles, contract_step, 0)
 
         for k in range(n):
-            part[k] = acc[k * band : (k + 1) * band, :].astype(BF16)
-        for k in range(1, n):
-            part_copy(k).start()
+            part[k % 2, k // 2] = acc[k * band : (k + 1) * band, :].astype(BF16)
+        side_copy().start()
 
         @pl.when(later)
         def _():
@@ -473,6 +488,13 @@
 
         for c in range(chunks):
             lay(parity, vir, c)
+        side_copy().wait_recv()
+        for k in range(line_size):
+            both = acc[own_band(k), :] + side_in[k].astype(F32)
+            acc[own_band(k), :] = both
+            line[k] = both.astype(BF16)
+        for k in range(1, line_size):
+            line_copy(k).start()
         lax.fori_loop(0, chunks, active_base, 0)
 
         @pl.when(jnp.logical_not(later))
@@ -487,14 +509,17 @@
                         couple[j, side].astype(F32).T.astype(BF16)
                     )
 
-        total = acc[pl.ds(pl.multiple_of(vir * band, band), band), :]
-        for k in range(1, n):
-            total = total + parts[part_landed(k)].astype(F32)
+        total = acc[own_band(level), :]
+        for k in range(1, line_size):
+            total = total + line_in[line_landed(k)].astype(F32)
         whole[vir] = total.astype(BF16)
-        for k in range(1, n):
+        for k in range(line_size):
             whole_copy(k).start()
         for c in range(chunks):
             lay(parity, landed(parity, 0 if c < split else 1, half, c), c)
+        for k in range(1, line_size):
+            whole_landed(k)
+            pass_copy(k, lane_side).start()
         heights = virtual.shape[0]
         padded = -(-heights // 16) * 16
 
@@ -514,8 +539,9 @@
                 for stage in range(1, half + 1):
                     if stage < half or sent_last(side, c):
                         hop(parity, side, stage, c).wait_send()
-        for k in range(1, n):
-            whole_landed(k)
+        whole_landed(0)
+        for k in range(1, line_size):
+            pass_copy(k, 1 - lane_side).wait_recv()
         block = depth
         for width in (512, 384, 256, 128):
             if depth % width == 0:
@@ -525,8 +551,11 @@
             cols = whole[:, :, q : q + block].reshape(lanes, block).astype(F32).T
             inter[q : q + block, :] = cols.astype(BF16)
             turned[q : q + block, :] = turn(cols, pairs).astype(BF16)
-        for k in range(1, n):
-            part_copy(k).wait_send()
+        side_copy().wait_send()
+        for k in range(1, line_size):
+            line_copy(k).wait_send()
+            pass_copy(k, lane_side).wait_send()
+        for k in range(line_size):
             whole_copy(k).wait_send()
 
         final = p == PASSES - 1
@@ -601,8 +630,8 @@
         couple_copy(k).wait_send()
 
 
-FIRST_RELAYS = {1: 8, 2: 9, 3: 10, 5: 16, 6: 17, 7: 18, 9: 24, 10: 25, 11: 26}
-LATER_RELAYS = {0: 9, 3: 24, 4: 17, 6: 10, 7: 25, 8: 18, 10: 26}
+FIRST_RELAYS = {2: 8, 4: 9, 5: 10, 6: 16, 7: 17, 8: 18, 9: 24, 10: 25, 11: 26}
+LATER_RELAYS = {1: 9, 4: 24, 5: 17, 7: 10, 8: 25, 9: 18, 11: 26}
 
 
 def all_passes(fit_rows, source, give, eps, row, act, n):
@@ -615,7 +644,7 @@
     span = wide // (chunks * n)
     half = n // 2
     dma = pltpu.SemaphoreType.DMA
-    band = pltpu.VMEM((n, lanes // n, depth), BF16)
+    line = pltpu.VMEM((n // 2, lanes // n, depth), BF16)
     each = pltpu.VMEM((chunks, tile, lanes), BF16)
     twice = pltpu.VMEM((chunks, 2, tile, lanes), BF16)
     state = pltpu.VMEM((chunks, tile, lanes), F32)
@@ -632,9 +661,11 @@
             pltpu.VMEM((SLOTS, 2, tile, depth), BF16),
             dma((SLOTS,)),
             pltpu.VMEM((lanes, depth), F32),
-            band,
-            band,
-            band,
+            pltpu.VMEM((2, n // 2, lanes // n, depth), BF16),
+            line,
+            line,
+            line,
+            pltpu.VMEM((n, lanes // n, depth), BF16),
             pltpu.VMEM((depth, lanes), BF16),
             pltpu.VMEM((depth, lanes), BF16),
             pltpu.VMEM((2, n, chunks, tile, lanes), BF16),
@@ -657,7 +688,10 @@
             dma((2, half, chunks)),
             dma((2, half, chunks)),
         ]
-        + [dma((n - 1,))] * 4
+        + [dma((1,))] * 2
+        + [dma((n // 2 - 1,))] * 2
+        + [dma((n // 2,))] * 2
+        + [dma((n // 2 - 1,))] * 2
         + [dma((2, chunks))]
         + [dma((n_fit - 1,))] * 2
         + [dma((chunks, 2))] * 2

time: 254 us -> 252 us (level)
  no operation moved by 1% of the time
where the time goes in v4:
time: 252 us
  Pallas kernels  243 us (96%)
  local copies, waits for them, and re-layouts  6.37 us (3%)
    pallas_call x1, Pallas kernels, all_passes(): pl.pallas_call(lambda *refs: passes_kernel(n, *refs), in_specs=[any_space...  238 us
    pallas_call x1, Pallas kernels, epilogue(): pl.pallas_call(epilogue_kernel, grid=(pieces // CHUNKS,), in_specs=[pl.Bl...  5.8 us

profile of v4, /device:TPU:0, one launch (start us, length us, event | category | flops | bytes accessed | tf_op | source)
XLA Modules:
  0.0 252.1 jit_solution(9388647964151782293)
XLA Ops:
  0.0 0.7 broadcast_subtract_fusion
  0.7 0.7 pad_maximum_fusion.1.refs_4_.row_ref
  1.4 0.8 copy.11
  2.2 1.7 constant_dynamic-slice_fusion
  3.9 0.7 copy.9
  4.6 0.2 copy.12
  4.8 1.2 pad.4.clone
  6.0 0.1 multiply_bitcast_fusion
  6.2 0.3 reshape.57
  6.5 0.7 pad_maximum_fusion.refs_5_
  7.2 0.0 copy-start
  7.2 0.0 copy-start.2
  7.2 0.0 copy-start.3
  7.2 237.6 %passes.1 = bf16[3,4,600,128]{3,2,1,0:T(8,128)(2,1)} custom-call(bf16[2,7200,1792]{2,1,0:T(8,128)(2,1)} %bitcast.23, f32[7200,128]{1,0:T(8,128)} %bitcast.20, bf16[4,2,192,384]{3,2,1,0:T(8,128)(2,1)} %bitcast.24, f32[300]{0:T(512)} %eps_ref.1, f32[24,128]{1,0:T(8,128)} %pad_maximum_fusion.1.refs_4_.row_ref, bf16[2,120,240]{2,1,0:T(8,128)(2,1)} %pad_maximum_fusion.refs_5_), custom_call_target="tpu_custom_call" | custom-call | tf_op jit(solution)/shard_map/passes/pallas_call | solution.py:652
  244.8 0.0 copy-done
  244.8 0.0 copy-done.2
  244.8 0.0 copy-done.3
  244.8 0.0 copy-start.1
  244.8 1.5 copy-done.1
  246.3 5.8 %epilogue.1 = f32[7200,128]{1,0:T(8,128)} custom-call(f32[300]{0:T(512)S(1)} %copy-done.3, f32[24,128]{1,0:T(8,128)S(1)} %copy-done.2, f32[7200,128]{1,0:T(8,128)S(1)} %bitcast.21, bf16[12,600,128]{2,1,0:T(8,128)(2,1)S(1)} %bitcast.22), custom_call_target="tpu_custom_call" | custom-call | tf_op jit(solution)/shard_map/epilogue/pallas_call | solution.py:123
  (2 shorter events, 0.0 us)
Async XLA Ops:
  7.2 237.6 %copy-start = (f32[2,300,1536]{2,0,1:T(2,128)S(1)}, f32[2,300,1536]{2,0,1:T(2,128)}, u32[]{:S(2)}) copy-start(f32[2,300,1536]{2,0,1:T(2,128)} %param.13) | copy-start | bytes 11059204
  7.2 237.6 %copy-start.2 = (f32[24,128]{1,0:T(8,128)S(1)}, f32[24,128]{1,0:T(8,128)}, u32[]{:S(2)}) copy-start(f32[24,128]{1,0:T(8,128)} %pad_maximum_fusion.1.refs_4_.row_ref) | copy-start | bytes 36868
  7.2 237.6 %copy-start.3 = (f32[300]{0:T(512)S(1)}, f32[300]{0:T(512)}, u32[]{:S(2)}) copy-start(f32[300]{0:T(512)} %eps_ref.1) | copy-start | bytes 3604
  244.8 1.5 copy-start.1
